TPU v7x, 512 devices: a whole 4x8x8 slice. The times are simulated.
512 devices in a mesh: dp: 32 (over z_lo, y, core), blk: 16 (over z_hi, x).
Axes of the slice: x: 4, y: 8, z: 8 (z_hi: 4, z_lo: 2; z = z_hi * 2 + z_lo), core: 2. Of those that a mesh axis runs over, the one named last changes fastest.
Arguments:
- hidden_in: bfloat16 [12288, 1152], P(('dp', 'blk')), may hold values from -6 to 6
- gain_mlp: float32 [1152], replicated, may hold values from 0.1 to 1.9
- gain_final: float32 [1152], replicated, may hold values from 0.1 to 1.9
- w_in: bfloat16 [1152, 4304], P(None, 'blk'), may hold values from -0.1875 to 0.1875
- w_out: bfloat16 [4304, 1152], P('blk'), may hold values from -0.09375 to 0.09375
- image_embeds: bfloat16 [12288, 1152], P(('dp', 'blk')), may hold values from -6 to 6
- pair_ids: int32 [12288], P(('dp', 'blk')), may hold values from 0 to 383
- teacher_logits: bfloat16 [32, 384, 384], P('dp', None, 'blk'), may hold values from -12 to 12
Outputs:
- grad_hidden: float32 [12288, 1152], P(('dp', 'blk'))
- grad_w_in: float32 [1152, 4304], P(None, 'blk')
- grad_w_out: float32 [4304, 1152], P('blk')
All inputs are finite; a program needn't handle non-finite values.
Results may differ from a plain program's by a relative error of at most 0.0067.
Values may be sent and summed in bfloat16 or wider, within the bound.
No kernel may reach another device: no remote copies, remote signals or barrier semaphores. Data moves between devices by JAX's collectives and lax.ppermute only.
A program may use at most 64 MiB of HBM per device.

v0:
```python
import jax
import jax.numpy as jnp
from jax import lax
from jax.sharding import PartitionSpec as P

epsilon = 1e-06
logit_scale = 10.0
logit_bias = -2.0
gelu_coeff = 0.7978845608028654


def from_behind(x, axis, by):
    length = lax.axis_size(axis)
    return lax.ppermute(x, axis, [(i, (i + by) % length) for i in range(length)])


def layer_norm(values, gain_vec):
    row_mean = jnp.mean(values, axis=-1, keepdims=True)
    centred = values - row_mean
    variance = jnp.mean(centred * centred, axis=-1, keepdims=True)
    inverse = lax.rsqrt(variance + epsilon)
    normed = centred * inverse
    return (normed, inverse, normed * gain_vec)


def norm_backward(grad_normed, normed, inverse):
    mean_grad = jnp.mean(grad_normed, axis=-1, keepdims=True)
    mean_cross = jnp.mean(grad_normed * normed, axis=-1, keepdims=True)
    return inverse * (grad_normed - mean_grad - normed * mean_cross)


def gelu_both(pre_act):
    inner_arg = gelu_coeff * (pre_act + 0.044715 * pre_act * pre_act * pre_act)
    tangent = jnp.tanh(inner_arg)
    gelu_value = 0.5 * pre_act * (1.0 + tangent)
    gelu_slope = 0.5 * (1.0 + tangent) + 0.5 * pre_act * (1.0 - tangent * tangent) * gelu_coeff * (
        1.0 + 3.0 * 0.044715 * pre_act * pre_act
    )
    return (gelu_value, gelu_slope)


def tile_grad(image_rows, image_ids, text_rows, text_ids, teacher_tile):
    logits = lax.dot_general(
        image_rows, text_rows, (((1,), (1,)), ((), ())), preferred_element_type=jnp.float32
    )
    logits = logits * logit_scale + logit_bias
    same_pair = (image_ids[:, None] == text_ids[None, :]).astype(jnp.float32)
    target = 0.5 * same_pair + 0.5 * jax.nn.sigmoid(teacher_tile.astype(jnp.float32))
    pair_grad = (jax.nn.sigmoid(logits) - target).astype(jnp.bfloat16)
    return lax.dot_general(
        pair_grad, image_rows, (((0,), (0,)), ((), ())), preferred_element_type=jnp.float32
    )


def per_device(
    hidden_in, gain_mlp, gain_final, w_in, w_out, image_embeds, pair_ids, teacher_logits
):
    row_count = hidden_in.shape[0]
    width = hidden_in.shape[1]
    blocks = lax.axis_size("blk")
    own_index = lax.axis_index("blk")
    hidden = hidden_in.astype(jnp.float32)
    normed_in, inverse_in, scaled_in = layer_norm(hidden, gain_mlp)
    mlp_input = scaled_in.astype(jnp.bfloat16)
    group_input = lax.all_gather(mlp_input, "blk", axis=0, tiled=True)
    pre_act = jnp.dot(group_input, w_in, preferred_element_type=jnp.float32)
    gelu_value, gelu_slope = gelu_both(pre_act)
    activation = gelu_value.astype(jnp.bfloat16)
    piece = activation
    residual = hidden + lax.psum_scatter(
        jnp.dot(piece, w_out, preferred_element_type=jnp.float32),
        "blk",
        scatter_dimension=0,
        tiled=True,
    )
    normed_out, inverse_out, final_out = layer_norm(residual, gain_final)
    length = jnp.sqrt(jnp.sum(final_out * final_out, axis=-1, keepdims=True) + epsilon)
    unit_text = final_out / length
    text_embed = unit_text.astype(jnp.bfloat16)
    image_float = image_embeds.astype(jnp.float32)
    image_unit = (
        image_float
        * lax.rsqrt(jnp.sum(image_float * image_float, axis=-1, keepdims=True) + epsilon)
    ).astype(jnp.bfloat16)
    group_ids = lax.all_gather(pair_ids, "blk", axis=0, tiled=True)
    teacher_cols = teacher_logits[0]
    empty_grads = jnp.zeros((row_count, width), jnp.float32)

    def rotate_once(turn_index, loop_state):
        text_rows, teacher_block, text_grads = loop_state
        source = (own_index - turn_index + blocks) % blocks
        text_ids = lax.dynamic_slice_in_dim(group_ids, source * row_count, row_count, 0)
        teacher_tile = lax.dynamic_slice_in_dim(teacher_block, own_index * row_count, row_count, 0)
        text_grads = text_grads + tile_grad(image_unit, pair_ids, text_rows, text_ids, teacher_tile)
        text_rows, teacher_block = from_behind((text_rows, teacher_block), "blk", 1)
        text_grads = from_behind(text_grads, "blk", 1)
        return (text_rows, teacher_block, text_grads)

    loop_state = lax.fori_loop(0, blocks, rotate_once, (text_embed, teacher_cols, empty_grads))
    text_grad = logit_scale * loop_state[2]
    radial = jnp.sum(unit_text * text_grad, axis=-1, keepdims=True)
    grad_final = (text_grad - unit_text * radial) / length
    grad_residual = norm_backward(grad_final * gain_final, normed_out, inverse_out)
    residual_rows = grad_residual.astype(jnp.bfloat16)
    group_grads = lax.all_gather(residual_rows, "blk", axis=0, tiled=True)
    grad_activation = lax.dot_general(
        group_grads, w_out, (((1,), (1,)), ((), ())), preferred_element_type=jnp.float32
    )
    grad_pre = (grad_activation * gelu_slope).astype(jnp.bfloat16)
    part_w_out = lax.dot_general(
        activation, group_grads, (((0,), (0,)), ((), ())), preferred_element_type=jnp.float32
    )
    part_w_in = lax.dot_general(
        group_input, grad_pre, (((0,), (0,)), ((), ())), preferred_element_type=jnp.float32
    )
    piece = grad_pre
    grad_input_norm = lax.psum_scatter(
        lax.dot_general(piece, w_in, (((1,), (1,)), ((), ())), preferred_element_type=jnp.float32),
        "blk",
        scatter_dimension=0,
        tiled=True,
    )
    grad_w_in, grad_w_out = lax.psum((part_w_in, part_w_out), "dp")
    grad_hidden = grad_residual + norm_backward(grad_input_norm * gain_mlp, normed_in, inverse_in)
    return (grad_hidden, grad_w_in, grad_w_out)


def solution(mesh):
    in_specs = (
        P(("dp", "blk"), None),
        P(),
        P(),
        P(None, "blk"),
        P("blk", None),
        P(("dp", "blk"), None),
        P(("dp", "blk")),
        P("dp", None, "blk"),
    )
    out_specs = (P(("dp", "blk"), None), P(None, "blk"), P("blk", None))
    return jax.shard_map(
        per_device, mesh=mesh, in_specs=in_specs, out_specs=out_specs, check_vma=False
    )
```

profile of v0, /device:TPU:1, one launch (start us, length us, event | category | flops | bytes accessed | tf_op | source)
XLA Modules:
  0.0 792.6 jit_solution(666342185659985724)
XLA Ops:
  10.2 49.3 %all_gather.9 = bf16[384,1152]{1,0:T(8,128)(2,1)S(1)} all-gather(bf16[24,1152]{1,0:T(8,128)(2,1)S(1)} %fusion.41), channel_id=1, replica_groups=mesh['dp'=32,'blk'=16] {'blk'}, dimensions={0}, use_global_device_ids=true | all-gather | bytes 940032 | tf_op jit(solution)/shard_map/all_gather | solution.py:65
  60.0 1.9 fusion.50
  64.3 7.7 all-reduce
  72.1 86.8 %reduce-scatter.7.cloned.1.call-done = f32[24,1152]{1,0:T(8,128)} async-done(((f32[384,1152]{1,0:T(8,128)}), f32[24,1152]{1,0:T(8,128)}) %reduce-scatter.7.cloned.1.call-update) | async-done | bytes 110608
  160.5 222.1 %while.19 = (s32[]{:T(128)}, bf16[24,1152]{1,0:T(8,128)(2,1)S(1)}, bf16[384,24]{0,1:T(8,128)(2,1)S(1)}, f32[24,1152]{1,0:T(8,128)S(1)}, bf16[24,1152]{1,0:T(8,12...) while((s32[]{:T(128)}, bf16[24,1152]{1,0:T(8,128)(2,1)S(1)}, ...), condition=%wide.region_8.9_spmd, body=%wide.region_7.8_spmd.sunk | while | flops 2690515 | bytes 1279616 | solution.py:99
  160.9 2.1 collective-permute-start.2
  163.1 2.8 collective-permute-start
  165.9 2.5 collective-permute-start.1
  168.4 6.8 collective-permute-done.1
  177.5 1.9 collective-permute-start
  181.4 7.3 collective-permute-done.1
  194.9 7.2 collective-permute-done.1
  208.3 6.8 collective-permute-done.1
  221.3 7.2 collective-permute-done.1
  234.7 6.8 collective-permute-done.1
  247.8 6.8 collective-permute-done.1
  256.9 2.0 collective-permute-start
  260.9 7.8 collective-permute-done.1
  274.9 7.3 collective-permute-done.1
  288.4 7.4 collective-permute-done.1
  302.0 9.7 %collective-permute-done.1 = bf16[384,24]{0,1:T(8,128)(2,1)S(1)} collective-permute-done((bf16[384,24]{0,1:T(8,128)(2,1)S(1)}, bf16[384,24]{0,1:T(8,128)(2,1)S(1)}, u32[]{:S(2)}, u32[]{:S(2)}) %collective-permute-start.1) | collective-permute-done | bytes 18464 | tf_op jit(solution)/shard_map/while/body/eval_jaxpr/ppermute | solution.py:14
  318.0 10.2 %collective-permute-done.1 = bf16[384,24]{0,1:T(8,128)(2,1)S(1)} collective-permute-done((bf16[384,24]{0,1:T(8,128)(2,1)S(1)}, bf16[384,24]{0,1:T(8,128)(2,1)S(1)}, u32[]{:S(2)}, u32[]{:S(2)}) %collective-permute-start.1) | collective-permute-done | bytes 18464 | tf_op jit(solution)/shard_map/while/body/eval_jaxpr/ppermute | solution.py:14
  332.4 2.1 collective-permute-start.1
  334.5 8.3 %collective-permute-done.1 = bf16[384,24]{0,1:T(8,128)(2,1)S(1)} collective-permute-done((bf16[384,24]{0,1:T(8,128)(2,1)S(1)}, bf16[384,24]{0,1:T(8,128)(2,1)S(1)}, u32[]{:S(2)}, u32[]{:S(2)}) %collective-permute-start.1) | collective-permute-done | bytes 18464 | tf_op jit(solution)/shard_map/while/body/eval_jaxpr/ppermute | solution.py:14
  349.1 6.8 collective-permute-done.1
  362.2 7.1 collective-permute-done.1
  371.6 2.1 collective-permute-start
  375.6 6.9 collective-permute-done.1
  383.1 41.1 %all_gather.11 = bf16[384,1152]{1,0:T(8,128)(2,1)S(1)} all-gather(bf16[24,1152]{1,0:T(8,128)(2,1)S(1)} %get-tuple-element.236), channel_id=1, replica_groups=mesh['dp'=32,'blk'=16] {'blk'}, dimensions={0}, use_global_device_ids=true | all-gather | bytes 940032 | tf_op jit(solution)/shard_map/all_gather | solution.py:105
  430.4 116.2 %reduce-scatter.9.cloned.1.call-done = f32[24,1152]{1,0:T(8,128)} async-done(((f32[384,1152]{1,0:T(8,128)}), f32[24,1152]{1,0:T(8,128)}) %reduce-scatter.9.cloned.1.call-update) | async-done | bytes 110608
  549.4 233.2 %all-reduce.6.cloned.1.call-done = (f32[1152,269]{0,1:T(8,128)}, f32[269,1152]{1,0:T(8,128)}) async-done(((f32[1152,269]{0,1:T(8,128)}, f32[269,1152]{1,0:T(8,128)}), (f32[1152,269]{0,1:T(8,128)}, f32[269,1152]{1,0:T(8,128)})) %all-reduce.6.cloned.1.call-update) | async-done | bytes 2479120 | tf_op jit(solution)/shard_map/psum | solution.py:123
  782.6 2.5 copy.28
  (196 shorter events, 102.7 us)
Async XLA Ops:
  7.2 151.7 %reduce-scatter.7.cloned.1.call-start = ((), (), s32[]{:S(2)}) async-start(), calls=%async_computation.2 | async-start | bytes 1880064
  62.0 484.6 %reduce-scatter.9.cloned.1.call-start = ((), (), s32[]{:S(2)}) async-start(), calls=%async_computation.3 | async-start | bytes 1880064
  160.9 14.2 %collective-permute-start.2 = (f32[24,1152]{1,0:T(8,128)S(1)}, f32[24,1152]{1,0:T(8,128)S(1)}, u32[]{:S(2)}, u32[]{:S(2)}) collective-permute-start(f32[24,1152]{1,0:T(8,128)S(1)} %convolution_add_fusion.2), channel_id=1, source_target_pairs={{0,1},{1,2},{2,3},{3,4},{4,5},{5,6},{6,7},{7,8},{8,9},{9,10},{10,1... | collective-permute-start | bytes 331784 | tf_op jit(solution)/shard_map/while/body/eval_jaxpr/ppermute | solution.py:14
  163.1 12.1 %collective-permute-start = (bf16[24,1152]{1,0:T(8,128)(2,1)S(1)}, bf16[24,1152]{1,0:T(8,128)(2,1)S(1)}, u32[]{:S(2)}, u32[]{:S(2)}) collective-permute-start(bf16[24,1152]{1,0:T(8,128)(2,1)S(1)} %copy.17), channel_id=1, source_target_pairs={{0,1},{1,2},{2,3},{3,4},{4,5},{5,6},{6,7},{7,8},{8,9},{9,10},{10,1... | collective-permute-start | bytes 165896 | tf_op jit(solution)/shard_map/while/body/eval_jaxpr/ppermute | solution.py:14
  175.6 13.1 %collective-permute-start.2 = (f32[24,1152]{1,0:T(8,128)S(1)}, f32[24,1152]{1,0:T(8,128)S(1)}, u32[]{:S(2)}, u32[]{:S(2)}) collective-permute-start(f32[24,1152]{1,0:T(8,128)S(1)} %convolution_add_fusion.2), channel_id=1, source_target_pairs={{0,1},{1,2},{2,3},{3,4},{4,5},{5,6},{6,7},{7,8},{8,9},{9,10},{10,1... | collective-permute-start | bytes 331784 | tf_op jit(solution)/shard_map/while/body/eval_jaxpr/ppermute | solution.py:14
  177.5 11.1 %collective-permute-start = (bf16[24,1152]{1,0:T(8,128)(2,1)S(1)}, bf16[24,1152]{1,0:T(8,128)(2,1)S(1)}, u32[]{:S(2)}, u32[]{:S(2)}) collective-permute-start(bf16[24,1152]{1,0:T(8,128)(2,1)S(1)} %copy.17), channel_id=1, source_target_pairs={{0,1},{1,2},{2,3},{3,4},{4,5},{5,6},{6,7},{7,8},{8,9},{9,10},{10,1... | collective-permute-start | bytes 165896 | tf_op jit(solution)/shard_map/while/body/eval_jaxpr/ppermute | solution.py:14
  189.1 13.0 %collective-permute-start.2 = (f32[24,1152]{1,0:T(8,128)S(1)}, f32[24,1152]{1,0:T(8,128)S(1)}, u32[]{:S(2)}, u32[]{:S(2)}) collective-permute-start(f32[24,1152]{1,0:T(8,128)S(1)} %convolution_add_fusion.2), channel_id=1, source_target_pairs={{0,1},{1,2},{2,3},{3,4},{4,5},{5,6},{6,7},{7,8},{8,9},{9,10},{10,1... | collective-permute-start | bytes 331784 | tf_op jit(solution)/shard_map/while/body/eval_jaxpr/ppermute | solution.py:14
  191.0 11.1 %collective-permute-start = (bf16[24,1152]{1,0:T(8,128)(2,1)S(1)}, bf16[24,1152]{1,0:T(8,128)(2,1)S(1)}, u32[]{:S(2)}, u32[]{:S(2)}) collective-permute-start(bf16[24,1152]{1,0:T(8,128)(2,1)S(1)} %copy.17), channel_id=1, source_target_pairs={{0,1},{1,2},{2,3},{3,4},{4,5},{5,6},{6,7},{7,8},{8,9},{9,10},{10,1... | collective-permute-start | bytes 165896 | tf_op jit(solution)/shard_map/while/body/eval_jaxpr/ppermute | solution.py:14
  202.5 12.6 %collective-permute-start.2 = (f32[24,1152]{1,0:T(8,128)S(1)}, f32[24,1152]{1,0:T(8,128)S(1)}, u32[]{:S(2)}, u32[]{:S(2)}) collective-permute-start(f32[24,1152]{1,0:T(8,128)S(1)} %convolution_add_fusion.2), channel_id=1, source_target_pairs={{0,1},{1,2},{2,3},{3,4},{4,5},{5,6},{6,7},{7,8},{8,9},{9,10},{10,1... | collective-permute-start | bytes 331784 | tf_op jit(solution)/shard_map/while/body/eval_jaxpr/ppermute | solution.py:14
  215.5 13.0 %collective-permute-start.2 = (f32[24,1152]{1,0:T(8,128)S(1)}, f32[24,1152]{1,0:T(8,128)S(1)}, u32[]{:S(2)}, u32[]{:S(2)}) collective-permute-start(f32[24,1152]{1,0:T(8,128)S(1)} %convolution_add_fusion.2), channel_id=1, source_target_pairs={{0,1},{1,2},{2,3},{3,4},{4,5},{5,6},{6,7},{7,8},{8,9},{9,10},{10,1... | collective-permute-start | bytes 331784 | tf_op jit(solution)/shard_map/while/body/eval_jaxpr/ppermute | solution.py:14
  217.5 11.0 %collective-permute-start = (bf16[24,1152]{1,0:T(8,128)(2,1)S(1)}, bf16[24,1152]{1,0:T(8,128)(2,1)S(1)}, u32[]{:S(2)}, u32[]{:S(2)}) collective-permute-start(bf16[24,1152]{1,0:T(8,128)(2,1)S(1)} %copy.17), channel_id=1, source_target_pairs={{0,1},{1,2},{2,3},{3,4},{4,5},{5,6},{6,7},{7,8},{8,9},{9,10},{10,1... | collective-permute-start | bytes 165896 | tf_op jit(solution)/shard_map/while/body/eval_jaxpr/ppermute | solution.py:14
  228.9 12.6 %collective-permute-start.2 = (f32[24,1152]{1,0:T(8,128)S(1)}, f32[24,1152]{1,0:T(8,128)S(1)}, u32[]{:S(2)}, u32[]{:S(2)}) collective-permute-start(f32[24,1152]{1,0:T(8,128)S(1)} %convolution_add_fusion.2), channel_id=1, source_target_pairs={{0,1},{1,2},{2,3},{3,4},{4,5},{5,6},{6,7},{7,8},{8,9},{9,10},{10,1... | collective-permute-start | bytes 331784 | tf_op jit(solution)/shard_map/while/body/eval_jaxpr/ppermute | solution.py:14
  242.0 12.6 %collective-permute-start.2 = (f32[24,1152]{1,0:T(8,128)S(1)}, f32[24,1152]{1,0:T(8,128)S(1)}, u32[]{:S(2)}, u32[]{:S(2)}) collective-permute-start(f32[24,1152]{1,0:T(8,128)S(1)} %convolution_add_fusion.2), channel_id=1, source_target_pairs={{0,1},{1,2},{2,3},{3,4},{4,5},{5,6},{6,7},{7,8},{8,9},{9,10},{10,1... | collective-permute-start | bytes 331784 | tf_op jit(solution)/shard_map/while/body/eval_jaxpr/ppermute | solution.py:14
  255.0 13.6 %collective-permute-start.2 = (f32[24,1152]{1,0:T(8,128)S(1)}, f32[24,1152]{1,0:T(8,128)S(1)}, u32[]{:S(2)}, u32[]{:S(2)}) collective-permute-start(f32[24,1152]{1,0:T(8,128)S(1)} %convolution_add_fusion.2), channel_id=1, source_target_pairs={{0,1},{1,2},{2,3},{3,4},{4,5},{5,6},{6,7},{7,8},{8,9},{9,10},{10,1... | collective-permute-start | bytes 331784 | tf_op jit(solution)/shard_map/while/body/eval_jaxpr/ppermute | solution.py:14
  256.9 11.7 %collective-permute-start = (bf16[24,1152]{1,0:T(8,128)(2,1)S(1)}, bf16[24,1152]{1,0:T(8,128)(2,1)S(1)}, u32[]{:S(2)}, u32[]{:S(2)}) collective-permute-start(bf16[24,1152]{1,0:T(8,128)(2,1)S(1)} %copy.17), channel_id=1, source_target_pairs={{0,1},{1,2},{2,3},{3,4},{4,5},{5,6},{6,7},{7,8},{8,9},{9,10},{10,1... | collective-permute-start | bytes 165896 | tf_op jit(solution)/shard_map/while/body/eval_jaxpr/ppermute | solution.py:14
  269.1 13.1 %collective-permute-start.2 = (f32[24,1152]{1,0:T(8,128)S(1)}, f32[24,1152]{1,0:T(8,128)S(1)}, u32[]{:S(2)}, u32[]{:S(2)}) collective-permute-start(f32[24,1152]{1,0:T(8,128)S(1)} %convolution_add_fusion.2), channel_id=1, source_target_pairs={{0,1},{1,2},{2,3},{3,4},{4,5},{5,6},{6,7},{7,8},{8,9},{9,10},{10,1... | collective-permute-start | bytes 331784 | tf_op jit(solution)/shard_map/while/body/eval_jaxpr/ppermute | solution.py:14
  271.0 11.1 %collective-permute-start = (bf16[24,1152]{1,0:T(8,128)(2,1)S(1)}, bf16[24,1152]{1,0:T(8,128)(2,1)S(1)}, u32[]{:S(2)}, u32[]{:S(2)}) collective-permute-start(bf16[24,1152]{1,0:T(8,128)(2,1)S(1)} %copy.17), channel_id=1, source_target_pairs={{0,1},{1,2},{2,3},{3,4},{4,5},{5,6},{6,7},{7,8},{8,9},{9,10},{10,1... | collective-permute-start | bytes 165896 | tf_op jit(solution)/shard_map/while/body/eval_jaxpr/ppermute | solution.py:14
  282.6 13.2 %collective-permute-start.2 = (f32[24,1152]{1,0:T(8,128)S(1)}, f32[24,1152]{1,0:T(8,128)S(1)}, u32[]{:S(2)}, u32[]{:S(2)}) collective-permute-start(f32[24,1152]{1,0:T(8,128)S(1)} %convolution_add_fusion.2), channel_id=1, source_target_pairs={{0,1},{1,2},{2,3},{3,4},{4,5},{5,6},{6,7},{7,8},{8,9},{9,10},{10,1... | collective-permute-start | bytes 331784 | tf_op jit(solution)/shard_map/while/body/eval_jaxpr/ppermute | solution.py:14
  284.5 11.2 %collective-permute-start = (bf16[24,1152]{1,0:T(8,128)(2,1)S(1)}, bf16[24,1152]{1,0:T(8,128)(2,1)S(1)}, u32[]{:S(2)}, u32[]{:S(2)}) collective-permute-start(bf16[24,1152]{1,0:T(8,128)(2,1)S(1)} %copy.17), channel_id=1, source_target_pairs={{0,1},{1,2},{2,3},{3,4},{4,5},{5,6},{6,7},{7,8},{8,9},{9,10},{10,1... | collective-permute-start | bytes 165896 | tf_op jit(solution)/shard_map/while/body/eval_jaxpr/ppermute | solution.py:14
  296.2 15.5 %collective-permute-start.2 = (f32[24,1152]{1,0:T(8,128)S(1)}, f32[24,1152]{1,0:T(8,128)S(1)}, u32[]{:S(2)}, u32[]{:S(2)}) collective-permute-start(f32[24,1152]{1,0:T(8,128)S(1)} %convolution_add_fusion.2), channel_id=1, source_target_pairs={{0,1},{1,2},{2,3},{3,4},{4,5},{5,6},{6,7},{7,8},{8,9},{9,10},{10,1... | collective-permute-start | bytes 331784 | tf_op jit(solution)/shard_map/while/body/eval_jaxpr/ppermute | solution.py:14
  298.1 13.6 %collective-permute-start = (bf16[24,1152]{1,0:T(8,128)(2,1)S(1)}, bf16[24,1152]{1,0:T(8,128)(2,1)S(1)}, u32[]{:S(2)}, u32[]{:S(2)}) collective-permute-start(bf16[24,1152]{1,0:T(8,128)(2,1)S(1)} %copy.17), channel_id=1, source_target_pairs={{0,1},{1,2},{2,3},{3,4},{4,5},{5,6},{6,7},{7,8},{8,9},{9,10},{10,1... | collective-permute-start | bytes 165896 | tf_op jit(solution)/shard_map/while/body/eval_jaxpr/ppermute | solution.py:14
  300.1 11.7 %collective-permute-start.1 = (bf16[384,24]{0,1:T(8,128)(2,1)S(1)}, bf16[384,24]{0,1:T(8,128)(2,1)S(1)}, u32[]{:S(2)}, u32[]{:S(2)}) collective-permute-start(bf16[384,24]{0,1:T(8,128)(2,1)S(1)} %copy.18), channel_id=1, source_target_pairs={{0,1},{1,2},{2,3},{3,4},{4,5},{5,6},{6,7},{7,8},{8,9},{9,10},{10,1... | collective-permute-start | bytes 55304 | tf_op jit(solution)/shard_map/while/body/eval_jaxpr/ppermute | solution.py:14
  312.2 16.0 %collective-permute-start.2 = (f32[24,1152]{1,0:T(8,128)S(1)}, f32[24,1152]{1,0:T(8,128)S(1)}, u32[]{:S(2)}, u32[]{:S(2)}) collective-permute-start(f32[24,1152]{1,0:T(8,128)S(1)} %convolution_add_fusion.2), channel_id=1, source_target_pairs={{0,1},{1,2},{2,3},{3,4},{4,5},{5,6},{6,7},{7,8},{8,9},{9,10},{10,1... | collective-permute-start | bytes 331784 | tf_op jit(solution)/shard_map/while/body/eval_jaxpr/ppermute | solution.py:14
  314.1 14.0 %collective-permute-start = (bf16[24,1152]{1,0:T(8,128)(2,1)S(1)}, bf16[24,1152]{1,0:T(8,128)(2,1)S(1)}, u32[]{:S(2)}, u32[]{:S(2)}) collective-permute-start(bf16[24,1152]{1,0:T(8,128)(2,1)S(1)} %copy.17), channel_id=1, source_target_pairs={{0,1},{1,2},{2,3},{3,4},{4,5},{5,6},{6,7},{7,8},{8,9},{9,10},{10,1... | collective-permute-start | bytes 165896 | tf_op jit(solution)/shard_map/while/body/eval_jaxpr/ppermute | solution.py:14
  316.0 12.1 %collective-permute-start.1 = (bf16[384,24]{0,1:T(8,128)(2,1)S(1)}, bf16[384,24]{0,1:T(8,128)(2,1)S(1)}, u32[]{:S(2)}, u32[]{:S(2)}) collective-permute-start(bf16[384,24]{0,1:T(8,128)(2,1)S(1)} %copy.18), channel_id=1, source_target_pairs={{0,1},{1,2},{2,3},{3,4},{4,5},{5,6},{6,7},{7,8},{8,9},{9,10},{10,1... | collective-permute-start | bytes 55304 | tf_op jit(solution)/shard_map/while/body/eval_jaxpr/ppermute | solution.py:14
  328.6 14.3 %collective-permute-start.2 = (f32[24,1152]{1,0:T(8,128)S(1)}, f32[24,1152]{1,0:T(8,128)S(1)}, u32[]{:S(2)}, u32[]{:S(2)}) collective-permute-start(f32[24,1152]{1,0:T(8,128)S(1)} %convolution_add_fusion.2), channel_id=1, source_target_pairs={{0,1},{1,2},{2,3},{3,4},{4,5},{5,6},{6,7},{7,8},{8,9},{9,10},{10,1... | collective-permute-start | bytes 331784 | tf_op jit(solution)/shard_map/while/body/eval_jaxpr/ppermute | solution.py:14
  330.5 12.4 %collective-permute-start = (bf16[24,1152]{1,0:T(8,128)(2,1)S(1)}, bf16[24,1152]{1,0:T(8,128)(2,1)S(1)}, u32[]{:S(2)}, u32[]{:S(2)}) collective-permute-start(bf16[24,1152]{1,0:T(8,128)(2,1)S(1)} %copy.17), channel_id=1, source_target_pairs={{0,1},{1,2},{2,3},{3,4},{4,5},{5,6},{6,7},{7,8},{8,9},{9,10},{10,1... | collective-permute-start | bytes 165896 | tf_op jit(solution)/shard_map/while/body/eval_jaxpr/ppermute | solution.py:14
  343.3 12.6 %collective-permute-start.2 = (f32[24,1152]{1,0:T(8,128)S(1)}, f32[24,1152]{1,0:T(8,128)S(1)}, u32[]{:S(2)}, u32[]{:S(2)}) collective-permute-start(f32[24,1152]{1,0:T(8,128)S(1)} %convolution_add_fusion.2), channel_id=1, source_target_pairs={{0,1},{1,2},{2,3},{3,4},{4,5},{5,6},{6,7},{7,8},{8,9},{9,10},{10,1... | collective-permute-start | bytes 331784 | tf_op jit(solution)/shard_map/while/body/eval_jaxpr/ppermute | solution.py:14
  356.4 12.9 %collective-permute-start.2 = (f32[24,1152]{1,0:T(8,128)S(1)}, f32[24,1152]{1,0:T(8,128)S(1)}, u32[]{:S(2)}, u32[]{:S(2)}) collective-permute-start(f32[24,1152]{1,0:T(8,128)S(1)} %convolution_add_fusion.2), channel_id=1, source_target_pairs={{0,1},{1,2},{2,3},{3,4},{4,5},{5,6},{6,7},{7,8},{8,9},{9,10},{10,1... | collective-permute-start | bytes 331784 | tf_op jit(solution)/shard_map/while/body/eval_jaxpr/ppermute | solution.py:14
  369.7 12.9 %collective-permute-start.2 = (f32[24,1152]{1,0:T(8,128)S(1)}, f32[24,1152]{1,0:T(8,128)S(1)}, u32[]{:S(2)}, u32[]{:S(2)}) collective-permute-start(f32[24,1152]{1,0:T(8,128)S(1)} %convolution_add_fusion.2), channel_id=1, source_target_pairs={{0,1},{1,2},{2,3},{3,4},{4,5},{5,6},{6,7},{7,8},{8,9},{9,10},{10,1... | collective-permute-start | bytes 331784 | tf_op jit(solution)/shard_map/while/body/eval_jaxpr/ppermute | solution.py:14
  371.6 11.0 %collective-permute-start = (bf16[24,1152]{1,0:T(8,128)(2,1)S(1)}, bf16[24,1152]{1,0:T(8,128)(2,1)S(1)}, u32[]{:S(2)}, u32[]{:S(2)}) collective-permute-start(bf16[24,1152]{1,0:T(8,128)(2,1)S(1)} %copy.17), channel_id=1, source_target_pairs={{0,1},{1,2},{2,3},{3,4},{4,5},{5,6},{6,7},{7,8},{8,9},{9,10},{10,1... | collective-permute-start | bytes 165896 | tf_op jit(solution)/shard_map/while/body/eval_jaxpr/ppermute | solution.py:14
  427.2 355.4 %all-reduce.6.cloned.1.call-start = ((), (), s32[]{:S(2)}) async-start(), calls=%async_computation.4 | async-start | bytes 5013504 | tf_op jit(solution)/shard_map/psum | solution.py:123
  (29 other events, 712.2 us)
Sparse Core Ops, SparseCore 0:
  62.1 96.6 reduce-scatter.6
  427.3 119.2 reduce-scatter.8
  550.2 232.2 all-reduce.5
where the time goes:
time: 795 us; the launch traced here: 793 us
  waiting for transfers between devices  557 us (70%)
  blocking collectives  98 us (12%)
  starting transfers between devices  94.3 us (12%)
  between operations  14.5 us (2%)
  matrix products  13.3 us (2%)
    psum x1, waiting for transfers between devices, per_device(): grad_w_in, grad_w_out = lax.psum((part_w_in, part_w_out), 'dp')  233 us
    unnamed x5, waiting for transfers between devices  203 us
    ppermute x48, waiting for transfers between devices, from_behind(): lax.ppermute(x, axis, [(i, (i + by) % length) for i in range(length)])  120 us
    ppermute x48, starting transfers between devices, from_behind(): lax.ppermute(x, axis, [(i, (i + by) % length) for i in range(length)])  94.2 us
    all_gather x1, blocking collectives, per_device(): group_input = lax.all_gather(mlp_input, 'blk', axis=0, tiled=True)  49.3 us
    all_gather x1, blocking collectives, per_device(): group_grads = lax.all_gather(residual_rows, 'blk', axis=0, tiled=True)  41.1 us
  transfers between devices with their start and end apart: 51, of which 19 were waited for; matrix products, arithmetic and copies ran while one was open for 1% of the time, Pallas kernels for 0%

commit v1 on v0

v1 whole, which is shorter than its diff:
```python
import jax
import jax.numpy as jnp
from jax import lax
from jax.sharding import Mesh
from jax.sharding import PartitionSpec as P

epsilon = 1e-06
logit_scale = 10.0
logit_bias = -2.0
gelu_coeff = 0.7978845608028654

DP = ("zl", "y", "co")
BLK = ("zh", "x")
RING = ("zl", "y")
LANES = 128


def layer_norm(values, gain_vec):
    row_mean = jnp.mean(values, axis=-1, keepdims=True)
    centred = values - row_mean
    variance = jnp.mean(centred * centred, axis=-1, keepdims=True)
    inverse = lax.rsqrt(variance + epsilon)
    normed = centred * inverse
    return (normed, inverse, normed * gain_vec)


def norm_backward(grad_normed, normed, inverse):
    mean_grad = jnp.mean(grad_normed, axis=-1, keepdims=True)
    mean_cross = jnp.mean(grad_normed * normed, axis=-1, keepdims=True)
    return inverse * (grad_normed - mean_grad - normed * mean_cross)


def gelu_both(pre_act):
    inner_arg = gelu_coeff * (pre_act + 0.044715 * pre_act * pre_act * pre_act)
    tangent = jnp.tanh(inner_arg)
    gelu_value = 0.5 * pre_act * (1.0 + tangent)
    gelu_slope = 0.5 * (1.0 + tangent) + 0.5 * pre_act * (1.0 - tangent * tangent) * gelu_coeff * (
        1.0 + 3.0 * 0.044715 * pre_act * pre_act
    )
    return (gelu_value, gelu_slope)


def to_all(block, axes):
    count = lax.axis_size(axes)
    copies = jnp.broadcast_to(block[None], (count,) + block.shape)
    return lax.all_to_all(copies, axes, 0, 0)


def pack(grad):
    rows = grad.shape[0]
    width = grad.shape[1]
    blocks = width // LANES
    tall = grad.reshape(rows, blocks, LANES).transpose(1, 0, 2).reshape(rows * blocks, LANES)
    return tall.astype(jnp.bfloat16)


def unpack(tall, rows, width):
    blocks = width // LANES
    grad = tall[: rows * blocks].reshape(blocks, rows, LANES).transpose(1, 0, 2)
    return grad.reshape(rows, width).astype(jnp.float32)


def per_device(
    hidden_in, gain_mlp, gain_final, w_in, w_out, image_embeds, pair_ids, teacher_logits
):
    row_count, width = hidden_in.shape
    units = w_in.shape[1]
    blocks = lax.axis_size(BLK)
    group = row_count * blocks
    hidden = hidden_in.astype(jnp.float32)
    normed_in, inverse_in, scaled_in = layer_norm(hidden, gain_mlp)
    mlp_input = scaled_in.astype(jnp.bfloat16)

    image_float = image_embeds.astype(jnp.float32)
    image_unit = (
        image_float
        * lax.rsqrt(jnp.sum(image_float * image_float, axis=-1, keepdims=True) + epsilon)
    ).astype(jnp.bfloat16)
    id_cols = jnp.stack([pair_ids & 127, pair_ids >> 7], axis=1).astype(jnp.bfloat16)
    payload = jnp.concatenate(
        [image_unit, jnp.pad(id_cols, ((0, 0), (0, LANES - 2)))], axis=1
    )
    with jax.named_scope("img_z"):
        column = to_all(payload, "zh").reshape(-1, width + LANES)

    with jax.named_scope("ag1"):
        group_input = to_all(mlp_input, BLK).reshape(group, width)
    with jax.named_scope("img_x"):
        images = to_all(column, "x").reshape(group, width + LANES)
    pre_act = jnp.dot(group_input, w_in, preferred_element_type=jnp.float32)
    gelu_value, gelu_slope = gelu_both(pre_act)
    activation = gelu_value.astype(jnp.bfloat16)
    part_sum = jnp.dot(activation, w_out, preferred_element_type=jnp.float32).astype(jnp.bfloat16)
    with jax.named_scope("rs1"):
        parts = lax.all_to_all(part_sum.reshape(blocks, row_count, width), BLK, 0, 0)
    residual = hidden + jnp.sum(parts.astype(jnp.float32), axis=0)
    normed_out, inverse_out, final_out = layer_norm(residual, gain_final)
    length = jnp.sqrt(jnp.sum(final_out * final_out, axis=-1, keepdims=True) + epsilon)
    unit_text = final_out / length
    text_embed = unit_text.astype(jnp.bfloat16)

    image_rows = images[:, :width]
    image_low = images[:, width].astype(jnp.int32)
    image_high = images[:, width + 1].astype(jnp.int32)
    image_ids = image_high * 128 + image_low
    teacher = teacher_logits[0].T.reshape(row_count, 4, 4, row_count).transpose(0, 2, 1, 3)
    teacher = teacher.reshape(row_count, group).astype(jnp.float32)
    logits = lax.dot_general(
        text_embed, image_rows, (((1,), (1,)), ((), ())), preferred_element_type=jnp.float32
    )
    logits = logits * logit_scale + logit_bias
    same_pair = (pair_ids[:, None] == image_ids[None, :]).astype(jnp.float32)
    target = 0.5 * same_pair + 0.5 * jax.nn.sigmoid(teacher)
    pair_grad = (jax.nn.sigmoid(logits) - target).astype(jnp.bfloat16)
    text_grad = logit_scale * jnp.dot(pair_grad, image_rows, preferred_element_type=jnp.float32)
    radial = jnp.sum(unit_text * text_grad, axis=-1, keepdims=True)
    grad_final = (text_grad - unit_text * radial) / length
    grad_residual = norm_backward(grad_final * gain_final, normed_out, inverse_out)
    residual_rows = grad_residual.astype(jnp.bfloat16)
    with jax.named_scope("ag2"):
        group_grads = to_all(residual_rows, BLK).reshape(group, width)
    grad_activation = lax.dot_general(
        group_grads, w_out, (((1,), (1,)), ((), ())), preferred_element_type=jnp.float32
    )
    grad_pre = (grad_activation * gelu_slope).astype(jnp.bfloat16)
    part_w_out = lax.dot_general(
        activation, group_grads, (((0,), (0,)), ((), ())), preferred_element_type=jnp.float32
    )
    part_w_in = lax.dot_general(
        grad_pre, group_input, (((0,), (0,)), ((), ())), preferred_element_type=jnp.float32
    )
    part_norm = lax.dot_general(
        grad_pre, w_in, (((1,), (1,)), ((), ())), preferred_element_type=jnp.float32
    ).astype(jnp.bfloat16)

    both = jnp.stack([pack(part_w_out), pack(part_w_in)])
    tall = both.shape[1]
    ring = lax.axis_size(RING)
    chunk = -(-tall // (8 * ring)) * 8
    both = jnp.pad(both, ((0, 0), (0, chunk * ring - tall), (0, 0)))
    with jax.named_scope("rs_co"):
        pair = lax.all_to_all(both, "co", 0, 0)
    mine = (pair[0].astype(jnp.float32) + pair[1].astype(jnp.float32)).astype(jnp.bfloat16)
    with jax.named_scope("rs_dp"):
        slices = lax.all_to_all(mine.reshape(ring, chunk, LANES), RING, 0, 0)
    with jax.named_scope("rs2"):
        norm_parts = lax.all_to_all(part_norm.reshape(blocks, row_count, width), BLK, 0, 0)
    total = jnp.sum(slices.astype(jnp.float32), axis=0).astype(jnp.bfloat16)
    with jax.named_scope("ag_dp"):
        whole = to_all(total, RING).reshape(ring * chunk, LANES)
    with jax.named_scope("ag_co"):
        wholes = to_all(whole, "co")
    grad_w_out = unpack(wholes[0], units, width)
    grad_w_in = unpack(wholes[1], units, width).T

    grad_input_norm = jnp.sum(norm_parts.astype(jnp.float32), axis=0)
    grad_hidden = grad_residual + norm_backward(grad_input_norm * gain_mlp, normed_in, inverse_in)
    return (grad_hidden, grad_w_in, grad_w_out)


def solution(mesh):
    fine = Mesh(mesh.devices.reshape(2, 8, 2, 4, 4), ("zl", "y", "co", "zh", "x"))
    rows = DP + BLK
    in_specs = (
        P(rows, None),
        P(),
        P(),
        P(None, BLK),
        P(BLK, None),
        P(rows, None),
        P(rows),
        P(DP, None, BLK),
    )
    out_specs = (P(rows, None), P(None, BLK), P(BLK, None))
    return jax.shard_map(
        per_device, mesh=fine, in_specs=in_specs, out_specs=out_specs, check_vma=False
    )
```

time: 795 us -> 237 us (0.30)
  waiting for transfers between devices: 557 us -> 88.4 us
  blocking collectives: 98 us -> 47.3 us
  starting transfers between devices: 94.3 us -> 59 us
  local copies, waits for them, and re-layouts: 6.93 us -> 20.6 us
  between operations: 14.5 us -> 0.92 us
    psum x1 -> x0, waiting for transfers between devices: 233 us -> none  [per_device(): grad_w_in, grad_w_out = lax.psum((part_w_in, part_w_out), 'dp')]
    unnamed x5 -> x0, waiting for transfers between devices: 203 us -> none
    ppermute x48 -> x0, waiting for transfers between devices: 120 us -> none  [from_behind(): lax.ppermute(x, axis, [(i, (i + by) % length) for i in range(length)])]
    ppermute x48 -> x0, starting transfers between devices: 94.2 us -> none  [from_behind(): lax.ppermute(x, axis, [(i, (i + by) % length) for i in range(length)])]
    all_gather x2 -> x0, blocking collectives: 90.3 us -> none  [the longest x1 49.3 us: per_device(): group_input = lax.all_gather(mlp_input, 'blk', axis=0, tiled=True)]
    all_to_all x0 -> x7, waiting for transfers between devices: none -> 88.4 us  [the longest x4 39.8 us: to_all(): return lax.all_to_all(copies, axes, 0, 0)]
    all_to_all x0 -> x7, starting transfers between devices: none -> 59 us  [the longest x4 30.1 us: to_all(): return lax.all_to_all(copies, axes, 0, 0)]
    all_to_all x0 -> x3, blocking collectives: none -> 47.3 us  [the longest x2 33.8 us: to_all(): return lax.all_to_all(copies, axes, 0, 0)]
  transfers between devices with their start and end apart: 51 -> 7, of which waited for: 19 -> 7; matrix products, arithmetic and copies ran while one was open for 1% -> 5% of each run, Pallas kernels for 0% -> 0%
where the time goes in v1:
time: 237 us; the launch traced here: 235 us
  waiting for transfers between devices  88.4 us (37%)
  starting transfers between devices  59 us (25%)
  blocking collectives  47.3 us (20%)
  local copies, waits for them, and re-layouts  20.6 us (9%)
  other arithmetic  10.7 us (5%)
  matrix products  8.44 us (4%)
    all_to_all x4, waiting for transfers between devices, to_all(): return lax.all_to_all(copies, axes, 0, 0)  39.8 us
    all_to_all x2, blocking collectives, to_all(): return lax.all_to_all(copies, axes, 0, 0)  33.8 us
    all_to_all x4, starting transfers between devices, to_all(): return lax.all_to_all(copies, axes, 0, 0)  30.1 us
    all_to_all x1, waiting for transfers between devices, per_device(): lax.all_to_all(part_norm.reshape(blocks, row_count, width), BLK, 0, 0)  23.7 us
    all_to_all x1, starting transfers between devices, per_device(): slices = lax.all_to_all(mine.reshape(ring, chunk, LANES), RING, 0, 0)  17.4 us
    all_to_all x1, waiting for transfers between devices, per_device(): slices = lax.all_to_all(mine.reshape(ring, chunk, LANES), RING, 0, 0)  14.8 us
    all_to_all x1, blocking collectives, per_device(): pair = lax.all_to_all(both, 'co', 0, 0)  13.5 us
    all_to_all x1, waiting for transfers between devices, per_device(): lax.all_to_all(part_sum.reshape(blocks, row_count, width), BLK, 0, 0)  10.1 us
  transfers between devices with their start and end apart: 7, of which 7 were waited for; matrix products, arithmetic and copies ran while one was open for 5% of the time, Pallas kernels for 0%

profile of v1, /device:TPU:1, one launch (start us, length us, event | category | flops | bytes accessed | tf_op | source)
XLA Modules:
  0.0 235.4 jit_solution(15666306067764960020)
XLA Ops:
  0.7 1.0 fusion.34
  4.1 10.8 %all-to-all-start.2 = ((bf16[4,24,1280]{2,1,0:T(8,128)(2,1)}), bf16[4,24,1280]{2,1,0:T(8,128)(2,1)S(1)}, u32[]{:S(2)}, u32[]{:S(2)}) async-start(bf16[4,24,1280]{2,1,0:T(8,128)(2,1)} %broadcast_in_dim.17), calls=%async_computation.2 | async-start | bytes 491520 | tf_op jit(solution)/shard_map/img_z/all_to_all | solution.py:46
  15.8 1.0 fusion.33
  17.7 5.3 %all-to-all-done.2 = bf16[4,24,1280]{2,1,0:T(8,128)(2,1)S(1)} async-done(((bf16[4,24,1280]{2,1,0:T(8,128)(2,1)}), bf16[4,24,1280]{2,1,0:T(8,128)(2,1)S(1)}, u32[]{:S(2)}, u32[]{:S(2)}) %all-to-all-start.2) | async-done | bytes 245792 | tf_op jit(solution)/shard_map/img_z/all_to_all | solution.py:46
  23.0 27.0 %all_to_all.50 = bf16[16,24,1152]{2,1,0:T(8,128)(2,1)S(1)} all-to-all(bf16[16,24,1152]{2,1,0:T(8,128)(2,1)S(1)} %broadcast_in_dim.16), channel_id=1, replica_groups=mesh['zl'=2,'y'=8,'co'=2,'zh'=4,'x'=4] {'zh','x'}, dimensions={0} | all-to-all | bytes 1769472 | tf_op jit(solution)/shard_map/ag1/all_to_all | solution.py:46
  51.0 3.6 %all-to-all-start.3 = ((bf16[4,96,1280]{2,1,0:T(8,128)(2,1)}), bf16[4,96,1280]{2,1,0:T(8,128)(2,1)S(1)}, u32[]{:S(2)}, u32[]{:S(2)}) async-start(bf16[4,96,1280]{2,1,0:T(8,128)(2,1)} %broadcast_in_dim.19), calls=%async_computation.3 | async-start | bytes 1966080 | tf_op jit(solution)/shard_map/img_x/all_to_all | solution.py:46
  55.9 1.6 convolution_convert_fusion.1
  57.6 6.4 %all-to-all-done.3 = bf16[4,96,1280]{2,1,0:T(8,128)(2,1)S(1)} async-done(((bf16[4,96,1280]{2,1,0:T(8,128)(2,1)}), bf16[4,96,1280]{2,1,0:T(8,128)(2,1)S(1)}, u32[]{:S(2)}, u32[]{:S(2)}) %all-to-all-start.3) | async-done | bytes 983072 | tf_op jit(solution)/shard_map/img_x/all_to_all | solution.py:46
  64.0 6.2 %all-to-all-start.1 = ((bf16[16,24,1152]{2,1,0:T(8,128)(2,1)}), bf16[16,24,1152]{2,1,0:T(8,128)(2,1)S(1)}, u32[]{:S(2)}, u32[]{:S(2)}) async-start(bf16[16,24,1152]{2,1,0:T(8,128)(2,1)} %bitcast.63), calls=%async_computation.1 | async-start | bytes 1769472 | tf_op jit(solution)/shard_map/rs1/all_to_all | solution.py:95
  71.2 1.7 copy.33
  72.9 1.1 reshape.172
  74.2 10.1 %all-to-all-done.1 = bf16[16,24,1152]{2,1,0:T(8,128)(2,1)S(1)} async-done(((bf16[16,24,1152]{2,1,0:T(8,128)(2,1)}), bf16[16,24,1152]{2,1,0:T(8,128)(2,1)S(1)}, u32[]{:S(2)}, u32[]{:S(2)}) %all-to-all-start.1) | async-done | bytes 884768 | tf_op jit(solution)/shard_map/rs1/all_to_all | solution.py:95
  87.9 6.3 %all-to-all-start.4 = ((bf16[16,24,1152]{2,1,0:T(8,128)(2,1)}), bf16[16,24,1152]{2,1,0:T(8,128)(2,1)S(1)}, u32[]{:S(2)}, u32[]{:S(2)}) async-start(bf16[16,24,1152]{2,1,0:T(8,128)(2,1)} %broadcast_in_dim.20), calls=%async_computation.4 | async-start | bytes 1769472 | tf_op jit(solution)/shard_map/ag2/all_to_all | solution.py:46
  95.1 13.1 %all-to-all-done.4 = bf16[16,24,1152]{2,1,0:T(8,128)(2,1)S(1)} async-done(((bf16[16,24,1152]{2,1,0:T(8,128)(2,1)}), bf16[16,24,1152]{2,1,0:T(8,128)(2,1)S(1)}, u32[]{:S(2)}, u32[]{:S(2)}) %all-to-all-start.4) | async-done | bytes 884768 | tf_op jit(solution)/shard_map/ag2/all_to_all | solution.py:46
  108.2 1.6 fusion.5
  110.7 1.6 fusion.2
  113.3 13.5 %all_to_all.51 = bf16[2,2432,128]{2,1,0:T(8,128)(2,1)S(1)} all-to-all(bf16[2,2432,128]{2,1,0:T(8,128)(2,1)S(1)} %fusion.4), channel_id=1, replica_groups=mesh['zl'=2,'y'=8,'co'=2,'zh'=4,'x'=4] {'co'}, dimensions={0} | all-to-all | bytes 2490368 | tf_op jit(solution)/shard_map/rs_co/all_to_all | solution.py:142
  127.8 17.4 %all-to-all-start.7 = ((bf16[16,152,128]{2,1,0:T(8,128)(2,1)}), bf16[16,152,128]{2,1,0:T(8,128)(2,1)S(1)}, u32[]{:S(2)}, u32[]{:S(2)}) async-start(bf16[16,152,128]{2,1,0:T(8,128)(2,1)} %bitcast.19), calls=%async_computation.7 | async-start | bytes 1245184 | tf_op jit(solution)/shard_map/rs_dp/all_to_all | solution.py:145
  145.2 1.6 convolution_convert_fusion
  146.8 14.8 %all-to-all-done.7 = bf16[16,152,128]{2,1,0:T(8,128)(2,1)S(1)} async-done(((bf16[16,152,128]{2,1,0:T(8,128)(2,1)}), bf16[16,152,128]{2,1,0:T(8,128)(2,1)S(1)}, u32[]{:S(2)}, u32[]{:S(2)}) %all-to-all-start.7) | async-done | bytes 622624 | tf_op jit(solution)/shard_map/rs_dp/all_to_all | solution.py:145
  161.5 5.4 %all-to-all-start.5 = ((bf16[16,24,1152]{2,1,0:T(8,128)(2,1)}), bf16[16,24,1152]{2,1,0:T(8,128)(2,1)S(1)}, u32[]{:S(2)}, u32[]{:S(2)}) async-start(bf16[16,24,1152]{2,1,0:T(8,128)(2,1)} %bitcast.10), calls=%async_computation.5 | async-start | bytes 1769472 | tf_op jit(solution)/shard_map/rs2/all_to_all | solution.py:147
  167.0 23.7 %all-to-all-done.5 = bf16[16,24,1152]{2,1,0:T(8,128)(2,1)S(1)} async-done(((bf16[16,24,1152]{2,1,0:T(8,128)(2,1)}), bf16[16,24,1152]{2,1,0:T(8,128)(2,1)S(1)}, u32[]{:S(2)}, u32[]{:S(2)}) %all-to-all-start.5) | async-done | bytes 884768 | tf_op jit(solution)/shard_map/rs2/all_to_all | solution.py:147
  191.7 9.3 %all-to-all-start.8 = ((bf16[16,152,128]{2,1,0:T(8,128)(2,1)}), bf16[16,152,128]{2,1,0:T(8,128)(2,1)S(1)}, u32[]{:S(2)}, u32[]{:S(2)}) async-start(bf16[16,152,128]{2,1,0:T(8,128)(2,1)} %broadcast_in_dim.21), calls=%async_computation.8 | async-start | bytes 1245184 | tf_op jit(solution)/shard_map/ag_dp/all_to_all | solution.py:46
  202.1 15.0 %all-to-all-done.8 = bf16[16,152,128]{2,1,0:T(8,128)(2,1)S(1)} async-done(((bf16[16,152,128]{2,1,0:T(8,128)(2,1)}), bf16[16,152,128]{2,1,0:T(8,128)(2,1)S(1)}, u32[]{:S(2)}, u32[]{:S(2)}) %all-to-all-start.8) | async-done | bytes 622624 | tf_op jit(solution)/shard_map/ag_dp/all_to_all | solution.py:46
  217.1 6.9 %all_to_all.52 = bf16[2,2432,128]{2,1,0:T(8,128)(2,1)S(1)} all-to-all(bf16[2,2432,128]{2,1,0:T(8,128)(2,1)S(1)} %broadcast_in_dim.23), channel_id=1, replica_groups=mesh['zl'=2,'y'=8,'co'=2,'zh'=4,'x'=4] {'co'}, dimensions={0} | all-to-all | bytes 2490368 | tf_op jit(solution)/shard_map/ag_co/all_to_all | solution.py:46
  224.0 1.2 slice_convert_fusion
  225.2 1.1 reshape.180
  226.3 1.8 copy.28
  228.2 1.6 copy.30
  229.7 2.3 reshape.184
  232.1 1.8 copy.27
  233.9 1.6 copy.29
  (64 shorter events, 17.1 us)
Async XLA Ops:
  0.6 55.3 %copy-start = (bf16[269,1152]{1,0:T(8,128)(2,1)S(1)}, bf16[269,1152]{1,0:T(8,128)(2,1)}, u32[]{:S(2)}) copy-start(bf16[269,1152]{1,0:T(8,128)(2,1)} %param.12) | copy-start | bytes 1859332
  0.6 16.2 %copy-start.3 = (bf16[24,1152]{1,0:T(8,128)(2,1)S(1)}, bf16[24,1152]{1,0:T(8,128)(2,1)}, u32[]{:S(2)}) copy-start(bf16[24,1152]{1,0:T(8,128)(2,1)} %param.8) | copy-start | bytes 165892
  4.1 18.9 %all-to-all-start.2 = ((bf16[4,24,1280]{2,1,0:T(8,128)(2,1)}), bf16[4,24,1280]{2,1,0:T(8,128)(2,1)S(1)}, u32[]{:S(2)}, u32[]{:S(2)}) async-start(bf16[4,24,1280]{2,1,0:T(8,128)(2,1)} %broadcast_in_dim.17), calls=%async_computation.2 | async-start | bytes 491520 | tf_op jit(solution)/shard_map/img_z/all_to_all | solution.py:46
  51.0 3.7 %copy-start.1 = (bf16[1152,269]{0,1:T(8,128)(2,1)S(1)}, bf16[1152,269]{0,1:T(8,128)(2,1)}, u32[]{:S(2)}) copy-start(bf16[1152,269]{0,1:T(8,128)(2,1)} %param.11) | copy-start | bytes 1859332
  51.0 13.0 %all-to-all-start.3 = ((bf16[4,96,1280]{2,1,0:T(8,128)(2,1)}), bf16[4,96,1280]{2,1,0:T(8,128)(2,1)S(1)}, u32[]{:S(2)}, u32[]{:S(2)}) async-start(bf16[4,96,1280]{2,1,0:T(8,128)(2,1)} %broadcast_in_dim.19), calls=%async_computation.3 | async-start | bytes 1966080 | tf_op jit(solution)/shard_map/img_x/all_to_all | solution.py:46
  55.2 0.7 copy-start.5
  57.6 12.6 %copy-start.8 = (bf16[1,384,24]{1,2,0:T(8,128)(2,1)S(1)}, bf16[1,384,24]{1,2,0:T(8,128)(2,1)}, u32[]{:S(2)}) copy-start(bf16[1,384,24]{1,2,0:T(8,128)(2,1)} %param.15) | copy-start | bytes 55300
  64.0 20.3 %all-to-all-start.1 = ((bf16[16,24,1152]{2,1,0:T(8,128)(2,1)}), bf16[16,24,1152]{2,1,0:T(8,128)(2,1)S(1)}, u32[]{:S(2)}, u32[]{:S(2)}) async-start(bf16[16,24,1152]{2,1,0:T(8,128)(2,1)} %bitcast.63), calls=%async_computation.1 | async-start | bytes 1769472 | tf_op jit(solution)/shard_map/rs1/all_to_all | solution.py:95
  70.2 14.6 %copy-start.7 = (f32[1152]{0:T(1024)S(1)}, f32[1152]{0:T(1024)}, u32[]{:S(2)}) copy-start(f32[1152]{0:T(1024)} %param.10) | copy-start | bytes 13828
  70.2 14.8 %copy-start.9 = (s32[24]{0:T(128)S(1)}, s32[24]{0:T(128)}, u32[]{:S(2)}) copy-start(s32[24]{0:T(128)} %param.14) | copy-start | bytes 292
  87.9 20.3 %all-to-all-start.4 = ((bf16[16,24,1152]{2,1,0:T(8,128)(2,1)}), bf16[16,24,1152]{2,1,0:T(8,128)(2,1)S(1)}, u32[]{:S(2)}, u32[]{:S(2)}) async-start(bf16[16,24,1152]{2,1,0:T(8,128)(2,1)} %broadcast_in_dim.20), calls=%async_computation.4 | async-start | bytes 1769472 | tf_op jit(solution)/shard_map/ag2/all_to_all | solution.py:46
  126.8 18.4 %copy-start.2 = (bf16[1152,269]{0,1:T(8,128)(2,1)S(1)}, bf16[1152,269]{0,1:T(8,128)(2,1)}, u32[]{:S(2)}) copy-start(bf16[1152,269]{0,1:T(8,128)(2,1)} %param.11) | copy-start | bytes 1859332
  127.8 33.7 %all-to-all-start.7 = ((bf16[16,152,128]{2,1,0:T(8,128)(2,1)}), bf16[16,152,128]{2,1,0:T(8,128)(2,1)S(1)}, u32[]{:S(2)}, u32[]{:S(2)}) async-start(bf16[16,152,128]{2,1,0:T(8,128)(2,1)} %bitcast.19), calls=%async_computation.7 | async-start | bytes 1245184 | tf_op jit(solution)/shard_map/rs_dp/all_to_all | solution.py:145
  161.5 29.2 %all-to-all-start.5 = ((bf16[16,24,1152]{2,1,0:T(8,128)(2,1)}), bf16[16,24,1152]{2,1,0:T(8,128)(2,1)S(1)}, u32[]{:S(2)}, u32[]{:S(2)}) async-start(bf16[16,24,1152]{2,1,0:T(8,128)(2,1)} %bitcast.10), calls=%async_computation.5 | async-start | bytes 1769472 | tf_op jit(solution)/shard_map/rs2/all_to_all | solution.py:147
  191.7 9.4 %copy-start.6 = (f32[1152]{0:T(1024)S(1)}, f32[1152]{0:T(1024)}, u32[]{:S(2)}) copy-start(f32[1152]{0:T(1024)} %param.9) | copy-start | bytes 13828
  191.7 9.7 %copy-start.4 = (f32[24,1152]{1,0:T(8,128)S(1)}, f32[24,1152]{1,0:T(8,128)}, u32[]{:S(2)}) copy-start(f32[24,1152]{1,0:T(8,128)} %get-tuple-element.14) | copy-start | bytes 331780
  191.7 25.4 %all-to-all-start.8 = ((bf16[16,152,128]{2,1,0:T(8,128)(2,1)}), bf16[16,152,128]{2,1,0:T(8,128)(2,1)S(1)}, u32[]{:S(2)}, u32[]{:S(2)}) async-start(bf16[16,152,128]{2,1,0:T(8,128)(2,1)} %broadcast_in_dim.21), calls=%async_computation.8 | async-start | bytes 1245184 | tf_op jit(solution)/shard_map/ag_dp/all_to_all | solution.py:46

commit v2 on v0

v2 whole, which is shorter than its diff:
```python
import jax
import jax.numpy as jnp
from jax import lax
from jax.experimental import pallas as pl
from jax.experimental.pallas import tpu as pltpu
from jax.sharding import Mesh
from jax.sharding import PartitionSpec as P


epsilon = 1e-06
logit_scale = 10.0
logit_bias = -2.0
gelu_coeff = 0.7978845608028654

DP = ("zl", "y", "co")
BLK = ("zh", "x")
RING = ("zl", "y")
LANES = 128
VMEM_GRANT = 8 * 2**20
F32 = jnp.float32
BF16 = jnp.bfloat16

NT = (((1,), (1,)), ((), ()))
TN = (((0,), (0,)), ((), ()))
NN = (((1,), (0,)), ((), ()))


def shape(dims, dtype):
    return jax.ShapeDtypeStruct(dims, dtype)


def call(body, outs, *args, scratch=(), flops=0):
    size = sum(a.size * a.dtype.itemsize for a in args)
    size += sum(o.size * o.dtype.itemsize for o in outs)
    near = pl.BlockSpec(memory_space=pltpu.VMEM)
    return pl.pallas_call(
        body,
        out_shape=tuple(outs),
        in_specs=[near] * len(args),
        out_specs=tuple([near] * len(outs)),
        scratch_shapes=list(scratch),
        compiler_params=pltpu.CompilerParams(vmem_limit_bytes=VMEM_GRANT),
        cost_estimate=pl.CostEstimate(flops=flops, bytes_accessed=size, transcendentals=0),
    )(*args)


def dot(a, b, dims):
    return lax.dot_general(a, b, dims, preferred_element_type=F32)


def norm_parts(values):
    row_mean = jnp.mean(values, axis=-1, keepdims=True)
    centred = values - row_mean
    variance = jnp.mean(centred * centred, axis=-1, keepdims=True)
    inverse = lax.rsqrt(variance + epsilon)
    return centred * inverse, inverse


def norm_backward(grad_normed, normed, inverse):
    mean_grad = jnp.mean(grad_normed, axis=-1, keepdims=True)
    mean_cross = jnp.mean(grad_normed * normed, axis=-1, keepdims=True)
    return inverse * (grad_normed - mean_grad - normed * mean_cross)


def gelu_both(pre_act):
    inner_arg = gelu_coeff * (pre_act + 0.044715 * pre_act * pre_act * pre_act)
    tangent = jnp.tanh(inner_arg)
    gelu_value = 0.5 * pre_act * (1.0 + tangent)
    gelu_slope = 0.5 * (1.0 + tangent) + 0.5 * pre_act * (1.0 - tangent * tangent) * gelu_coeff * (
        1.0 + 3.0 * 0.044715 * pre_act * pre_act
    )
    return gelu_value, gelu_slope


def text_in(hidden_ref, gain_ref, out_ref):
    normed, _ = norm_parts(hidden_ref[...].astype(F32))
    rows = (normed * gain_ref[...]).astype(BF16)
    for k in range(out_ref.shape[0]):
        out_ref[k] = rows


def column_of(row_ref):
    count = row_ref.shape[1]
    spread = jnp.broadcast_to(row_ref[...], (count, count))
    down = lax.broadcasted_iota(jnp.int32, (count, count), 0)
    along = lax.broadcasted_iota(jnp.int32, (count, count), 1)
    return jnp.sum(jnp.where(down == along, spread, 0), axis=1, keepdims=True)


def image_in(image_ref, id_ref, out_ref):
    image = image_ref[...].astype(F32)
    width = image.shape[1]
    scale = lax.rsqrt(jnp.sum(image * image, axis=-1, keepdims=True) + epsilon)
    out_ref[:, :width] = (image * scale).astype(BF16)
    ids = column_of(id_ref)
    lane = lax.broadcasted_iota(jnp.int32, (image.shape[0], LANES), 1)
    low = jnp.where(lane == 0, ids & 127, 0)
    high = jnp.where(lane == 1, ids >> 7, 0)
    out_ref[:, width:] = (low + high).astype(F32).astype(BF16)


def image_column(p0, p1, p2, p3, out_ref):
    at = lax.axis_index("zh")
    for k, piece in enumerate((p0, p1, p2, p3)):
        out_ref[lax.rem(at + 4 - k, 4)] = piece[...]


def image_all(q0, q1, q2, q3, teacher_ref, id_ref, image_ref, target_ref, tags):
    at = lax.axis_index("x")
    width = image_ref.shape[2]
    rows = image_ref.shape[1]
    for k, piece in enumerate((q0, q1, q2, q3)):
        x = lax.rem(at + 4 - k, 4)
        for z in range(4):
            image_ref[z * 4 + x] = piece[z, :, :width]
            tags[z * 4 + x] = piece[z, :, width:].astype(F32)
    marks = tags[...].reshape(16 * rows, LANES).astype(BF16)
    row = lax.broadcasted_iota(jnp.int32, (8, LANES), 0)
    lane = lax.broadcasted_iota(jnp.int32, (8, LANES), 1)
    pick = jnp.where(row == lane, 1.0, 0.0).astype(BF16)
    ids = dot(pick, marks, NT)
    image_id = ids[0:1] + 128.0 * ids[1:2]
    text_id = column_of(id_ref).astype(F32)
    same = jnp.where(text_id == image_id, 0.5, 0.0)
    target_ref[...] = same + 0.5 * jax.nn.sigmoid(teacher_ref[...].astype(F32))


def forward(rows_ref, w_in_ref, w_out_ref, part_ref, act_ref, slope_ref):
    blocks, rows, width = part_ref.shape
    pre_act = dot(rows_ref[...].reshape(blocks * rows, width), w_in_ref[...], NT)
    value, slope = gelu_both(pre_act)
    act = value.astype(BF16)
    act_ref[...] = act
    slope_ref[...] = slope
    part_ref[...] = dot(act, w_out_ref[...], NN).astype(BF16).reshape(blocks, rows, width)


def middle(part_ref, hidden_ref, gain_ref, image_ref, target_ref, out_ref, grad_ref):
    blocks, rows, width = part_ref.shape
    total = part_ref[0].astype(F32)
    for k in range(1, blocks):
        total = total + part_ref[k].astype(F32)
    residual = hidden_ref[...].astype(F32) + total
    gain = gain_ref[...]
    normed, inverse = norm_parts(residual)
    final = normed * gain
    length = jnp.sqrt(jnp.sum(final * final, axis=-1, keepdims=True) + epsilon)
    unit = final / length
    images = image_ref[...].reshape(blocks * rows, width)
    logits = dot(unit.astype(BF16), images, NT) * logit_scale + logit_bias
    pair_grad = (jax.nn.sigmoid(logits) - target_ref[...]).astype(BF16)
    text_grad = logit_scale * dot(pair_grad, images, NN)
    radial = jnp.sum(unit * text_grad, axis=-1, keepdims=True)
    grad_final = (text_grad - unit * radial) / length
    grad = norm_backward(grad_final * gain, normed, inverse)
    grad_ref[...] = grad
    sent = grad.astype(BF16)
    for k in range(blocks):
        out_ref[k] = sent


def backward(rows_ref, w_out_ref, slope_ref, grad_ref):
    blocks, rows, width = rows_ref.shape
    grad_act = dot(rows_ref[...].reshape(blocks * rows, width), w_out_ref[...], NT)
    grad_ref[...] = (grad_act * slope_ref[...]).astype(BF16)


def input_grad(grad_ref, w_in_ref, k0, k1, k2, k3, held):
    at = lax.axis_index("x")
    held[...] = dot(grad_ref[...], w_in_ref[...], NN).astype(BF16).reshape(held.shape)
    for k, out in enumerate((k0, k1, k2, k3)):
        x = lax.rem(at + k, 4)
        for z in range(4):
            out[z] = held[z * 4 + x]


def packed(a_ref, b_ref, out_ref, units, step, width):
    a = a_ref[...]
    b = b_ref[...]
    b = b.reshape(a.shape[0], width)
    for c in range(width // LANES):
        tile = dot(a, b[:, c * LANES : (c + 1) * LANES], TN)
        out_ref[pl.ds(c * step, units), :] = tile.astype(out_ref.dtype)


def weight_grad(first, step, act_ref, grads_ref, pre_ref, rows_ref, out_ref):
    units = act_ref.shape[1]
    width = grads_ref.shape[2]
    core = lax.axis_index("co")
    out_ref[...] = jnp.zeros_like(out_ref)

    @pl.when(core == first)
    def _():
        packed(act_ref, grads_ref, out_ref, units, step, width)

    @pl.when(core != first)
    def _():
        packed(pre_ref, rows_ref, out_ref, units, step, width)


def join(kept_ref, got_ref, out_ref):
    ring, chunk, lanes = out_ref.shape
    total = kept_ref[...] + got_ref[...].astype(F32)
    out_ref[...] = total.astype(BF16).reshape(ring, chunk, lanes)


def ring_sum(slices_ref, out_ref):
    total = slices_ref[0].astype(F32)
    for k in range(1, slices_ref.shape[0]):
        total = total + slices_ref[k].astype(F32)
    sent = total.astype(BF16)
    for k in range(out_ref.shape[0]):
        out_ref[k] = sent


def unpack(step, mine_ref, other_ref, w_out_ref, w_in_ref):
    units, width = w_out_ref.shape
    core = lax.axis_index("co")

    def spread(src, dst):
        for c in range(width // LANES):
            dst[:, c * LANES : (c + 1) * LANES] = src[pl.ds(c * step, units), :].astype(F32)

    @pl.when(core == 0)
    def _():
        spread(mine_ref, w_out_ref)
        spread(other_ref, w_in_ref)

    @pl.when(core != 0)
    def _():
        spread(other_ref, w_out_ref)
        spread(mine_ref, w_in_ref)


def column_sum(k0, k1, k2, k3, keep_ref, s1, s2, s3, held):
    at = lax.axis_index("zh")
    total = k0[...].astype(F32) + k1[...].astype(F32)
    held[...] = total + k2[...].astype(F32) + k3[...].astype(F32)
    keep_ref[...] = held[at]
    for k, out in enumerate((s1, s2, s3)):
        out[...] = held[lax.rem(at + k + 1, 4)].astype(BF16)


def last(keep_ref, g1, g2, g3, hidden_ref, gain_ref, grad_ref, out_ref):
    total = keep_ref[...] + g1[...].astype(F32) + g2[...].astype(F32) + g3[...].astype(F32)
    normed, inverse = norm_parts(hidden_ref[...].astype(F32))
    out_ref[...] = grad_ref[...] + norm_backward(total * gain_ref[...], normed, inverse)


def shift(value, axis, by):
    length = lax.axis_size(axis)
    return lax.ppermute(value, axis, [(i, (i + by) % length) for i in range(length)])


def per_device(
    hidden_in, gain_mlp, gain_final, w_in, w_out, image_embeds, pair_ids, teacher_logits
):
    rows, width = hidden_in.shape
    units = w_in.shape[1]
    blocks = lax.axis_size(BLK)
    ring = lax.axis_size(RING)
    group = rows * blocks
    gain_mlp = gain_mlp.reshape(1, width)
    gain_final = gain_final.reshape(1, width)
    ids = pair_ids.reshape(1, rows)
    w_in_rows = w_in.T
    teacher = teacher_logits[0].T
    spread = shape((blocks, rows, width), BF16)
    matmul = 2 * group * units * width

    (copies,) = call(text_in, [spread], hidden_in, gain_mlp)
    group_input = lax.all_to_all(copies, BLK, 0, 0)

    (payload,) = call(image_in, [shape((rows, width + LANES), BF16)], image_embeds, ids)
    near = [shift(payload, "zh", k) for k in (1, 2, 3)]
    (column,) = call(image_column, [shape((4, rows, width + LANES), BF16)], payload, *near)
    far = [shift(column, "x", k) for k in (1, 2, 3)]
    images, target = call(
        image_all,
        [spread, shape((rows, group), F32)],
        column,
        *far,
        teacher,
        ids,
        scratch=[pltpu.VMEM((blocks, rows, LANES), F32)],
    )

    part, act, slope = call(
        forward,
        [spread, shape((group, units), BF16), shape((group, units), F32)],
        group_input,
        w_in_rows,
        w_out,
        flops=2 * matmul,
    )
    parts = lax.all_to_all(part, BLK, 0, 0)
    copies, grad_residual = call(
        middle, [spread, shape((rows, width), F32)], parts, hidden_in, gain_final, images, target
    )
    group_grads = lax.all_to_all(copies, BLK, 0, 0)
    (grad_pre,) = call(
        backward, [shape((group, units), BF16)], group_grads, w_out, slope, flops=matmul
    )

    step = -(-units // 16) * 16
    chunk = -(-(step * (width // LANES)) // (8 * ring)) * 8
    tall = chunk * ring

    def grads(first, dtype):
        return call(
            lambda *refs: weight_grad(first, step, *refs),
            [shape((tall, LANES), dtype)],
            act,
            group_grads,
            grad_pre,
            group_input,
            flops=matmul,
        )[0]

    give = grads(1, BF16)
    got = shift(give, "co", 1)
    keep = grads(0, F32)
    (mine,) = call(join, [shape((ring, chunk, LANES), BF16)], keep, got)
    slices = lax.all_to_all(mine, RING, 0, 0)

    quarter = shape((4, rows, width), BF16)
    k0, s1, s2, s3 = call(
        input_grad,
        [quarter] * 4,
        grad_pre,
        w_in_rows,
        flops=matmul,
        scratch=[pltpu.VMEM((blocks, rows, width), BF16)],
    )
    arrived = [shift(s, "x", k + 1) for k, s in enumerate((s1, s2, s3))]
    own, s1, s2, s3 = call(
        column_sum,
        [shape((rows, width), F32)] + [shape((rows, width), BF16)] * 3,
        k0,
        *arrived,
        scratch=[pltpu.VMEM((4, rows, width), F32)],
    )
    arrived = [shift(s, "zh", k + 1) for k, s in enumerate((s1, s2, s3))]
    (grad_hidden,) = call(
        last, [shape((rows, width), F32)], own, *arrived, hidden_in, gain_mlp, grad_residual
    )

    (copies,) = call(ring_sum, [shape((ring, chunk, LANES), BF16)], slices)
    whole = lax.all_to_all(copies, RING, 0, 0).reshape(tall, LANES)
    other = shift(whole, "co", 1)
    grad_w_out, grad_w_in = call(
        lambda *refs: unpack(step, *refs), [shape((units, width), F32)] * 2, whole, other
    )
    return (grad_hidden, grad_w_in.T, grad_w_out)


def solution(mesh):
    fine = Mesh(mesh.devices.reshape(2, 8, 2, 4, 4), ("zl", "y", "co", "zh", "x"))
    every = DP + BLK
    in_specs = (
        P(every, None),
        P(),
        P(),
        P(None, BLK),
        P(BLK, None),
        P(every, None),
        P(every),
        P(DP, None, BLK),
    )
    out_specs = (P(every, None), P(None, BLK), P(BLK, None))
    return jax.shard_map(
        per_device, mesh=fine, in_specs=in_specs, out_specs=out_specs, check_vma=False
    )
```

time: 795 us -> 222 us (0.28)
  waiting for transfers between devices: 557 us -> 24.3 us
  starting transfers between devices: 94.3 us -> 67.7 us
  blocking collectives: 98 us -> 114 us
  between operations: 14.5 us -> 0.93 us
  matrix products: 13.3 us -> 0 us
  Pallas kernels: 0 us -> 9.54 us
    psum x1 -> x0, waiting for transfers between devices: 233 us -> none  [per_device(): grad_w_in, grad_w_out = lax.psum((part_w_in, part_w_out), 'dp')]
    unnamed x5 -> x0, waiting for transfers between devices: 203 us -> none
    all_to_all x0 -> x4, blocking collectives: none -> 114 us  [the longest x1 36.6 us: per_device(): slices = lax.all_to_all(mine, RING, 0, 0)]
    ppermute x48 -> x14, waiting for transfers between devices: 120 us -> 24.3 us  [shift(): lax.ppermute(value, axis, [(i, (i + by) % length) for i in range(length)])]
    all_gather x2 -> x0, blocking collectives: 90.3 us -> none  [the longest x1 49.3 us: per_device(): group_input = lax.all_gather(mlp_input, 'blk', axis=0, tiled=True)]
    ppermute x48 -> x14, starting transfers between devices: 94.2 us -> 61.3 us  [shift(): lax.ppermute(value, axis, [(i, (i + by) % length) for i in range(length)])]
    dot_general x22 -> x0, matrix products: 13.3 us -> none  [the longest x16 5.13 us: tile_grad(): lax.dot_general(pair_grad, image_rows, (((0,), (0,)), ((), ())), preferre...]
    pallas_call x0 -> x15, Pallas kernels: none -> 9.54 us  [call(): pl.pallas_call(body, out_shape=tuple(outs), in_specs=[near] * len(args),...]
  transfers between devices with their start and end apart: 51 -> 15, of which waited for: 19 -> 10; matrix products, arithmetic and copies ran while one was open for 1% -> 0% of each run, Pallas kernels for 0% -> 1%
where the time goes in v2:
time: 222 us; the launch traced here: 221 us
  blocking collectives  114 us (51%)
  starting transfers between devices  67.7 us (30%)
  waiting for transfers between devices  24.3 us (11%)
  Pallas kernels  9.54 us (4%)
  local copies, waits for them, and re-layouts  5.35 us (2%)
    ppermute x14, starting transfers between devices, shift(): lax.ppermute(value, axis, [(i, (i + by) % length) for i in range(length)])  61.3 us
    all_to_all x1, blocking collectives, per_device(): slices = lax.all_to_all(mine, RING, 0, 0)  36.6 us
    all_to_all x1, blocking collectives, per_device(): group_input = lax.all_to_all(copies, BLK, 0, 0)  33.2 us
    ppermute x14, waiting for transfers between devices, shift(): lax.ppermute(value, axis, [(i, (i + by) % length) for i in range(length)])  24.3 us
    all_to_all x1, blocking collectives, per_device(): whole = lax.all_to_all(copies, RING, 0, 0).reshape(tall, LANES)  22.8 us
    all_to_all x1, blocking collectives, per_device(): group_grads = lax.all_to_all(copies, BLK, 0, 0)  21 us
    pallas_call x15, Pallas kernels, call(): pl.pallas_call(body, out_shape=tuple(outs), in_specs=[near] * len(args),...  9.54 us
    all_to_all x1, starting transfers between devices, per_device(): parts = lax.all_to_all(part, BLK, 0, 0)  6.4 us
  transfers between devices with their start and end apart: 15, of which 10 were waited for; matrix products, arithmetic and copies ran while one was open for 0% of the time, Pallas kernels for 1%

profile of v2, /device:TPU:1, one launch (start us, length us, event | category | flops | bytes accessed | tf_op | source)
XLA Modules:
  0.0 221.3 jit_solution(17230975078554076552)
XLA Ops:
  2.4 33.2 %all_to_all.25.rows_ref.refs_3_ = bf16[16,24,1152]{2,1,0:T(8,128)(2,1)S(1)} all-to-all(bf16[16,24,1152]{2,1,0:T(8,128)(2,1)S(1)} %shard_map.103), channel_id=1, replica_groups=mesh['zl'=2,'y'=8,'co'=2,'zh'=4,'x'=4] {'zh','x'}, dimensions={0} | all-to-all | bytes 1769472 | tf_op jit(solution)/shard_map/all_to_all | solution.py:272
  35.6 1.5 shard_map.104
  38.8 6.4 %all-to-all-start.1 = ((bf16[16,24,1152]{2,1,0:T(8,128)(2,1)}), bf16[16,24,1152]{2,1,0:T(8,128)(2,1)S(1)}, u32[]{:S(2)}, u32[]{:S(2)}) async-start(bf16[16,24,1152]{2,1,0:T(8,128)(2,1)} %copy-done.2), calls=%async_computation.1 | async-start | bytes 1769472 | tf_op jit(solution)/shard_map/all_to_all | solution.py:296
  45.4 5.4 %collective-permute-start.2 = (bf16[24,1280]{1,0:T(8,128)(2,1)S(1)}, bf16[24,1280]{1,0:T(8,128)(2,1)S(1)}, u32[]{:S(2)}, u32[]{:S(2)}) collective-permute-start(bf16[24,1280]{1,0:T(8,128)(2,1)S(1)} %shard_map.105.p0), channel_id=1, source_target_pairs={{0,12},{4,0},{8,4},{12,8},{1,13},{5,1},{9,5},{13,9},{2,14},{6,2},{... | collective-permute-start | bytes 184328 | tf_op jit(solution)/shard_map/ppermute | solution.py:252
  50.8 4.0 %collective-permute-start.1 = (bf16[24,1280]{1,0:T(8,128)(2,1)S(1)}, bf16[24,1280]{1,0:T(8,128)(2,1)S(1)}, u32[]{:S(2)}, u32[]{:S(2)}) collective-permute-start(bf16[24,1280]{1,0:T(8,128)(2,1)S(1)} %shard_map.105.p0), channel_id=1, source_target_pairs={{0,8},{4,12},{8,0},{12,4},{1,9},{5,13},{9,1},{13,5},{2,10},{6,14},... | collective-permute-start | bytes 184328 | tf_op jit(solution)/shard_map/ppermute | solution.py:252
  54.8 4.0 %collective-permute-start = (bf16[24,1280]{1,0:T(8,128)(2,1)S(1)}, bf16[24,1280]{1,0:T(8,128)(2,1)S(1)}, u32[]{:S(2)}, u32[]{:S(2)}) collective-permute-start(bf16[24,1280]{1,0:T(8,128)(2,1)S(1)} %shard_map.105.p0), channel_id=1, source_target_pairs={{0,4},{4,8},{8,12},{12,0},{1,5},{5,9},{9,13},{13,1},{2,6},{6,10},{... | collective-permute-start | bytes 184328 | tf_op jit(solution)/shard_map/ppermute | solution.py:252
  58.8 3.8 %collective-permute-done.1.p2 = bf16[24,1280]{1,0:T(8,128)(2,1)S(1)} collective-permute-done((bf16[24,1280]{1,0:T(8,128)(2,1)S(1)}, bf16[24,1280]{1,0:T(8,128)(2,1)S(1)}, u32[]{:S(2)}, u32[]{:S(2)}) %collective-permute-start.1) | collective-permute-done | bytes 61472 | tf_op jit(solution)/shard_map/ppermute | solution.py:252
  63.2 5.0 %collective-permute-start.5 = (bf16[4,24,1280]{2,1,0:T(8,128)(2,1)S(1)}, bf16[4,24,1280]{2,1,0:T(8,128)(2,1)S(1)}, u32[]{:S(2)}, u32[]{:S(2)}) collective-permute-start(bf16[4,24,1280]{2,1,0:T(8,128)(2,1)S(1)} %shard_map.106.q0), channel_id=1, source_target_pairs={{0,3},{1,0},{2,1},{3,2},{4,7},{5,4},{6,5},{7,6},{8,11},{9,8},{10,9... | collective-permute-start | bytes 737288 | tf_op jit(solution)/shard_map/ppermute | solution.py:252
  68.2 2.2 %collective-permute-start.4 = (bf16[4,24,1280]{2,1,0:T(8,128)(2,1)S(1)}, bf16[4,24,1280]{2,1,0:T(8,128)(2,1)S(1)}, u32[]{:S(2)}, u32[]{:S(2)}) collective-permute-start(bf16[4,24,1280]{2,1,0:T(8,128)(2,1)S(1)} %shard_map.106.q0), channel_id=1, source_target_pairs={{0,2},{1,3},{2,0},{3,1},{4,6},{5,7},{6,4},{7,5},{8,10},{9,11},{10,... | collective-permute-start | bytes 737288 | tf_op jit(solution)/shard_map/ppermute | solution.py:252
  70.4 2.8 %collective-permute-start.3 = (bf16[4,24,1280]{2,1,0:T(8,128)(2,1)S(1)}, bf16[4,24,1280]{2,1,0:T(8,128)(2,1)S(1)}, u32[]{:S(2)}, u32[]{:S(2)}) collective-permute-start(bf16[4,24,1280]{2,1,0:T(8,128)(2,1)S(1)} %shard_map.106.q0), channel_id=1, source_target_pairs={{0,1},{1,2},{2,3},{3,0},{4,5},{5,6},{6,7},{7,4},{8,9},{9,10},{10,1... | collective-permute-start | bytes 737288 | tf_op jit(solution)/shard_map/ppermute | solution.py:252
  73.2 3.5 %collective-permute-done.4.q2 = bf16[4,24,1280]{2,1,0:T(8,128)(2,1)S(1)} collective-permute-done((bf16[4,24,1280]{2,1,0:T(8,128)(2,1)S(1)}, bf16[4,24,1280]{2,1,0:T(8,128)(2,1)S(1)}, u32[]{:S(2)}, u32[]{:S(2)}) %collective-permute-start.4) | collective-permute-done | bytes 245792 | tf_op jit(solution)/shard_map/ppermute | solution.py:252
  76.7 2.6 %collective-permute-done.3.q1 = bf16[4,24,1280]{2,1,0:T(8,128)(2,1)S(1)} collective-permute-done((bf16[4,24,1280]{2,1,0:T(8,128)(2,1)S(1)}, bf16[4,24,1280]{2,1,0:T(8,128)(2,1)S(1)}, u32[]{:S(2)}, u32[]{:S(2)}) %collective-permute-start.3) | collective-permute-done | bytes 245792 | tf_op jit(solution)/shard_map/ppermute | solution.py:252
  80.4 1.2 copy-done.4
  81.6 1.3 shard_map.108
  82.9 21.0 %all_to_all.26.rows_ref.refs_1_ = bf16[16,24,1152]{2,1,0:T(8,128)(2,1)S(1)} all-to-all(bf16[16,24,1152]{2,1,0:T(8,128)(2,1)S(1)} %get-tuple-element.23), channel_id=1, replica_groups=mesh['zl'=2,'y'=8,'co'=2,'zh'=4,'x'=4] {'zh','x'}, dimensions={0} | all-to-all | bytes 1769472 | tf_op jit(solution)/shard_map/all_to_all | solution.py:300
  105.5 12.8 %collective-permute-start.12 = (bf16[2560,128]{1,0:T(8,128)(2,1)S(1)}, bf16[2560,128]{1,0:T(8,128)(2,1)S(1)}, u32[]{:S(2)}, u32[]{:S(2)}) collective-permute-start(bf16[2560,128]{1,0:T(8,128)(2,1)S(1)} %shard_map.114), channel_id=1, source_target_pairs={{0,16},{16,0},{1,17},{17,1},{2,18},{18,2},{3,19},{19,3},{4,20},{20... | collective-permute-start | bytes 1966088 | tf_op jit(solution)/shard_map/ppermute | solution.py:252
  120.2 36.6 %all_to_all.27.slices_ref = bf16[16,160,128]{2,1,0:T(8,128)(2,1)S(1)} all-to-all(bf16[16,160,128]{2,1,0:T(8,128)(2,1)S(1)} %shard_map.115), channel_id=1, replica_groups=mesh['zl'=2,'y'=8,'co'=2,'zh'=4,'x'=4] {'zl','y'}, dimensions={0} | all-to-all | bytes 1310720 | tf_op jit(solution)/shard_map/all_to_all | solution.py:324
  156.8 22.8 %all_to_all.28 = bf16[16,160,128]{2,1,0:T(8,128)(2,1)S(1)} all-to-all(bf16[16,160,128]{2,1,0:T(8,128)(2,1)S(1)} %shard_map.116), channel_id=1, replica_groups=mesh['zl'=2,'y'=8,'co'=2,'zh'=4,'x'=4] {'zl','y'}, dimensions={0} | all-to-all | bytes 1310720 | tf_op jit(solution)/shard_map/all_to_all | solution.py:349
  179.6 5.4 %collective-permute-start.13 = (bf16[2560,128]{1,0:T(8,128)(2,1)S(1)}, bf16[2560,128]{1,0:T(8,128)(2,1)S(1)}, u32[]{:S(2)}, u32[]{:S(2)}) collective-permute-start(bf16[2560,128]{1,0:T(8,128)(2,1)S(1)} %bitcast.7), channel_id=1, source_target_pairs={{0,16},{16,0},{1,17},{17,1},{2,18},{18,2},{3,19},{19,3},{4,20},{20... | collective-permute-start | bytes 1966088 | tf_op jit(solution)/shard_map/ppermute | solution.py:252
  185.8 1.9 collective-permute-start.6
  187.7 4.1 %collective-permute-start.7 = (bf16[4,24,1152]{2,1,0:T(8,128)(2,1)S(1)}, bf16[4,24,1152]{2,1,0:T(8,128)(2,1)S(1)}, u32[]{:S(2)}, u32[]{:S(2)}) collective-permute-start(bf16[4,24,1152]{2,1,0:T(8,128)(2,1)S(1)} %get-tuple-element.27), channel_id=1, source_target_pairs={{0,2},{1,3},{2,0},{3,1},{4,6},{5,7},{6,4},{7,5},{8,10},{9,11},{10,... | collective-permute-start | bytes 663560 | tf_op jit(solution)/shard_map/ppermute | solution.py:252
  191.8 3.4 %collective-permute-start.8 = (bf16[4,24,1152]{2,1,0:T(8,128)(2,1)S(1)}, bf16[4,24,1152]{2,1,0:T(8,128)(2,1)S(1)}, u32[]{:S(2)}, u32[]{:S(2)}) collective-permute-start(bf16[4,24,1152]{2,1,0:T(8,128)(2,1)S(1)} %get-tuple-element.28), channel_id=1, source_target_pairs={{0,3},{1,0},{2,1},{3,2},{4,7},{5,4},{6,5},{7,6},{8,11},{9,8},{10,9... | collective-permute-start | bytes 663560 | tf_op jit(solution)/shard_map/ppermute | solution.py:252
  195.2 1.2 collective-permute-done.6.k1
  196.3 3.8 %collective-permute-done.7.k2 = bf16[4,24,1152]{2,1,0:T(8,128)(2,1)S(1)} collective-permute-done((bf16[4,24,1152]{2,1,0:T(8,128)(2,1)S(1)}, bf16[4,24,1152]{2,1,0:T(8,128)(2,1)S(1)}, u32[]{:S(2)}, u32[]{:S(2)}) %collective-permute-start.7) | collective-permute-done | bytes 221216 | tf_op jit(solution)/shard_map/ppermute | solution.py:252
  200.1 2.7 %collective-permute-done.8.k3 = bf16[4,24,1152]{2,1,0:T(8,128)(2,1)S(1)} collective-permute-done((bf16[4,24,1152]{2,1,0:T(8,128)(2,1)S(1)}, bf16[4,24,1152]{2,1,0:T(8,128)(2,1)S(1)}, u32[]{:S(2)}, u32[]{:S(2)}) %collective-permute-start.8) | collective-permute-done | bytes 221216 | tf_op jit(solution)/shard_map/ppermute | solution.py:252
  203.0 2.9 %collective-permute-start.9 = (bf16[24,1152]{1,0:T(8,128)(2,1)S(1)}, bf16[24,1152]{1,0:T(8,128)(2,1)S(1)}, u32[]{:S(2)}, u32[]{:S(2)}) collective-permute-start(bf16[24,1152]{1,0:T(8,128)(2,1)S(1)} %get-tuple-element.30), channel_id=1, source_target_pairs={{0,4},{4,8},{8,12},{12,0},{1,5},{5,9},{9,13},{13,1},{2,6},{6,10},{... | collective-permute-start | bytes 165896 | tf_op jit(solution)/shard_map/ppermute | solution.py:252
  205.9 2.2 collective-permute-start.10
  208.1 5.2 %collective-permute-start.11 = (bf16[24,1152]{1,0:T(8,128)(2,1)S(1)}, bf16[24,1152]{1,0:T(8,128)(2,1)S(1)}, u32[]{:S(2)}, u32[]{:S(2)}) collective-permute-start(bf16[24,1152]{1,0:T(8,128)(2,1)S(1)} %get-tuple-element.32), channel_id=1, source_target_pairs={{0,12},{4,0},{8,4},{12,8},{1,13},{5,1},{9,5},{13,9},{2,14},{6,2},{... | collective-permute-start | bytes 165896 | tf_op jit(solution)/shard_map/ppermute | solution.py:252
  213.3 1.4 collective-permute-done.10.g2
  214.8 4.0 %collective-permute-done.11.g3 = bf16[24,1152]{1,0:T(8,128)(2,1)S(1)} collective-permute-done((bf16[24,1152]{1,0:T(8,128)(2,1)S(1)}, bf16[24,1152]{1,0:T(8,128)(2,1)S(1)}, u32[]{:S(2)}, u32[]{:S(2)}) %collective-permute-start.11) | collective-permute-done | bytes 55328 | tf_op jit(solution)/shard_map/ppermute | solution.py:252
  218.8 0.9 shard_map.112
  219.7 1.6 shard_map.117
  (45 shorter events, 9.8 us)
Async XLA Ops:
  1.3 0.8 copy-start.7
  2.1 33.5 %copy-start = (bf16[269,1152]{1,0:T(8,128)(2,1)S(1)}, bf16[269,1152]{1,0:T(8,128)(2,1)}, u32[]{:S(2)}) copy-start(bf16[269,1152]{1,0:T(8,128)(2,1)} %w_out_ref.3) | copy-start | bytes 1859332
  2.1 33.5 %copy-start.1 = (bf16[1152,269]{0,1:T(8,128)(2,1)S(1)}, bf16[1152,269]{0,1:T(8,128)(2,1)}, u32[]{:S(2)}) copy-start(bf16[1152,269]{0,1:T(8,128)(2,1)} %param.11) | copy-start | bytes 1859332
  37.1 0.9 copy-start.2
  38.0 0.8 copy-start.5
  38.8 6.4 %copy-start.9 = (bf16[24,1152]{1,0:T(8,128)(2,1)S(1)}, bf16[24,1152]{1,0:T(8,128)(2,1)}, u32[]{:S(2)}) copy-start(bf16[24,1152]{1,0:T(8,128)(2,1)} %image_ref.1) | copy-start | bytes 165892
  38.8 6.4 %copy-start.11 = (s32[24]{0:T(128)S(1)}, s32[24]{0:T(128)}, u32[]{:S(2)}) copy-start(s32[24]{0:T(128)} %param.14) | copy-start | bytes 292
  38.8 34.3 %copy-start.12 = (f32[1152]{0:T(1024)S(1)}, f32[1152]{0:T(1024)}, u32[]{:S(2)}) copy-start(f32[1152]{0:T(1024)} %param.10) | copy-start | bytes 13828
  38.8 40.4 %copy-start.10 = (bf16[1,384,24]{1,2,0:T(8,128)(2,1)S(1)}, bf16[1,384,24]{1,2,0:T(8,128)(2,1)}, u32[]{:S(2)}) copy-start(bf16[1,384,24]{1,2,0:T(8,128)(2,1)} %param.15) | copy-start | bytes 55300
  38.8 41.6 %all-to-all-start.1 = ((bf16[16,24,1152]{2,1,0:T(8,128)(2,1)}), bf16[16,24,1152]{2,1,0:T(8,128)(2,1)S(1)}, u32[]{:S(2)}, u32[]{:S(2)}) async-start(bf16[16,24,1152]{2,1,0:T(8,128)(2,1)} %copy-done.2), calls=%async_computation.1 | async-start | bytes 1769472 | tf_op jit(solution)/shard_map/all_to_all | solution.py:296
  45.2 35.2 %copy-start.8 = (bf16[24,1152]{1,0:T(8,128)(2,1)S(1)}, bf16[24,1152]{1,0:T(8,128)(2,1)}, u32[]{:S(2)}) copy-start(bf16[24,1152]{1,0:T(8,128)(2,1)} %hidden_ref.5) | copy-start | bytes 165892
  45.4 13.4 %collective-permute-start.2 = (bf16[24,1280]{1,0:T(8,128)(2,1)S(1)}, bf16[24,1280]{1,0:T(8,128)(2,1)S(1)}, u32[]{:S(2)}, u32[]{:S(2)}) collective-permute-start(bf16[24,1280]{1,0:T(8,128)(2,1)S(1)} %shard_map.105.p0), channel_id=1, source_target_pairs={{0,12},{4,0},{8,4},{12,8},{1,13},{5,1},{9,5},{13,9},{2,14},{6,2},{... | collective-permute-start | bytes 184328 | tf_op jit(solution)/shard_map/ppermute | solution.py:252
  50.8 11.8 %collective-permute-start.1 = (bf16[24,1280]{1,0:T(8,128)(2,1)S(1)}, bf16[24,1280]{1,0:T(8,128)(2,1)S(1)}, u32[]{:S(2)}, u32[]{:S(2)}) collective-permute-start(bf16[24,1280]{1,0:T(8,128)(2,1)S(1)} %shard_map.105.p0), channel_id=1, source_target_pairs={{0,8},{4,12},{8,0},{12,4},{1,9},{5,13},{9,1},{13,5},{2,10},{6,14},... | collective-permute-start | bytes 184328 | tf_op jit(solution)/shard_map/ppermute | solution.py:252
  54.8 8.4 %collective-permute-start = (bf16[24,1280]{1,0:T(8,128)(2,1)S(1)}, bf16[24,1280]{1,0:T(8,128)(2,1)S(1)}, u32[]{:S(2)}, u32[]{:S(2)}) collective-permute-start(bf16[24,1280]{1,0:T(8,128)(2,1)S(1)} %shard_map.105.p0), channel_id=1, source_target_pairs={{0,4},{4,8},{8,12},{12,0},{1,5},{5,9},{9,13},{13,1},{2,6},{6,10},{... | collective-permute-start | bytes 184328 | tf_op jit(solution)/shard_map/ppermute | solution.py:252
  63.2 10.0 %collective-permute-start.5 = (bf16[4,24,1280]{2,1,0:T(8,128)(2,1)S(1)}, bf16[4,24,1280]{2,1,0:T(8,128)(2,1)S(1)}, u32[]{:S(2)}, u32[]{:S(2)}) collective-permute-start(bf16[4,24,1280]{2,1,0:T(8,128)(2,1)S(1)} %shard_map.106.q0), channel_id=1, source_target_pairs={{0,3},{1,0},{2,1},{3,2},{4,7},{5,4},{6,5},{7,6},{8,11},{9,8},{10,9... | collective-permute-start | bytes 737288 | tf_op jit(solution)/shard_map/ppermute | solution.py:252
  68.2 8.5 %collective-permute-start.4 = (bf16[4,24,1280]{2,1,0:T(8,128)(2,1)S(1)}, bf16[4,24,1280]{2,1,0:T(8,128)(2,1)S(1)}, u32[]{:S(2)}, u32[]{:S(2)}) collective-permute-start(bf16[4,24,1280]{2,1,0:T(8,128)(2,1)S(1)} %shard_map.106.q0), channel_id=1, source_target_pairs={{0,2},{1,3},{2,0},{3,1},{4,6},{5,7},{6,4},{7,5},{8,10},{9,11},{10,... | collective-permute-start | bytes 737288 | tf_op jit(solution)/shard_map/ppermute | solution.py:252
  70.4 8.9 %collective-permute-start.3 = (bf16[4,24,1280]{2,1,0:T(8,128)(2,1)S(1)}, bf16[4,24,1280]{2,1,0:T(8,128)(2,1)S(1)}, u32[]{:S(2)}, u32[]{:S(2)}) collective-permute-start(bf16[4,24,1280]{2,1,0:T(8,128)(2,1)S(1)} %shard_map.106.q0), channel_id=1, source_target_pairs={{0,1},{1,2},{2,3},{3,0},{4,5},{5,6},{6,7},{7,4},{8,9},{9,10},{10,1... | collective-permute-start | bytes 737288 | tf_op jit(solution)/shard_map/ppermute | solution.py:252
  79.5 0.9 copy-start.3
  80.4 1.2 copy-start.4
  82.9 21.0 %copy-start.6 = (f32[384,269]{1,0:T(8,128)S(1)}, f32[384,269]{1,0:T(8,128)}, u32[]{:S(2)}) copy-start(f32[384,269]{1,0:T(8,128)} %copy-done.5) | copy-start | bytes 1239556
  105.5 14.5 %collective-permute-start.12 = (bf16[2560,128]{1,0:T(8,128)(2,1)S(1)}, bf16[2560,128]{1,0:T(8,128)(2,1)S(1)}, u32[]{:S(2)}, u32[]{:S(2)}) collective-permute-start(bf16[2560,128]{1,0:T(8,128)(2,1)S(1)} %shard_map.114), channel_id=1, source_target_pairs={{0,16},{16,0},{1,17},{17,1},{2,18},{18,2},{3,19},{19,3},{4,20},{20... | collective-permute-start | bytes 1966088 | tf_op jit(solution)/shard_map/ppermute | solution.py:252
  179.6 40.1 %collective-permute-start.13 = (bf16[2560,128]{1,0:T(8,128)(2,1)S(1)}, bf16[2560,128]{1,0:T(8,128)(2,1)S(1)}, u32[]{:S(2)}, u32[]{:S(2)}) collective-permute-start(bf16[2560,128]{1,0:T(8,128)(2,1)S(1)} %bitcast.7), channel_id=1, source_target_pairs={{0,16},{16,0},{1,17},{17,1},{2,18},{18,2},{3,19},{19,3},{4,20},{20... | collective-permute-start | bytes 1966088 | tf_op jit(solution)/shard_map/ppermute | solution.py:252
  185.8 10.6 %collective-permute-start.6 = (bf16[4,24,1152]{2,1,0:T(8,128)(2,1)S(1)}, bf16[4,24,1152]{2,1,0:T(8,128)(2,1)S(1)}, u32[]{:S(2)}, u32[]{:S(2)}) collective-permute-start(bf16[4,24,1152]{2,1,0:T(8,128)(2,1)S(1)} %get-tuple-element.26), channel_id=1, source_target_pairs={{0,1},{1,2},{2,3},{3,0},{4,5},{5,6},{6,7},{7,4},{8,9},{9,10},{10,1... | collective-permute-start | bytes 663560 | tf_op jit(solution)/shard_map/ppermute | solution.py:252
  187.7 12.4 %collective-permute-start.7 = (bf16[4,24,1152]{2,1,0:T(8,128)(2,1)S(1)}, bf16[4,24,1152]{2,1,0:T(8,128)(2,1)S(1)}, u32[]{:S(2)}, u32[]{:S(2)}) collective-permute-start(bf16[4,24,1152]{2,1,0:T(8,128)(2,1)S(1)} %get-tuple-element.27), channel_id=1, source_target_pairs={{0,2},{1,3},{2,0},{3,1},{4,6},{5,7},{6,4},{7,5},{8,10},{9,11},{10,... | collective-permute-start | bytes 663560 | tf_op jit(solution)/shard_map/ppermute | solution.py:252
  191.8 11.0 %collective-permute-start.8 = (bf16[4,24,1152]{2,1,0:T(8,128)(2,1)S(1)}, bf16[4,24,1152]{2,1,0:T(8,128)(2,1)S(1)}, u32[]{:S(2)}, u32[]{:S(2)}) collective-permute-start(bf16[4,24,1152]{2,1,0:T(8,128)(2,1)S(1)} %get-tuple-element.28), channel_id=1, source_target_pairs={{0,3},{1,0},{2,1},{3,2},{4,7},{5,4},{6,5},{7,6},{8,11},{9,8},{10,9... | collective-permute-start | bytes 663560 | tf_op jit(solution)/shard_map/ppermute | solution.py:252
  203.0 10.3 %collective-permute-start.9 = (bf16[24,1152]{1,0:T(8,128)(2,1)S(1)}, bf16[24,1152]{1,0:T(8,128)(2,1)S(1)}, u32[]{:S(2)}, u32[]{:S(2)}) collective-permute-start(bf16[24,1152]{1,0:T(8,128)(2,1)S(1)} %get-tuple-element.30), channel_id=1, source_target_pairs={{0,4},{4,8},{8,12},{12,0},{1,5},{5,9},{9,13},{13,1},{2,6},{6,10},{... | collective-permute-start | bytes 165896 | tf_op jit(solution)/shard_map/ppermute | solution.py:252
  205.9 8.9 %collective-permute-start.10 = (bf16[24,1152]{1,0:T(8,128)(2,1)S(1)}, bf16[24,1152]{1,0:T(8,128)(2,1)S(1)}, u32[]{:S(2)}, u32[]{:S(2)}) collective-permute-start(bf16[24,1152]{1,0:T(8,128)(2,1)S(1)} %get-tuple-element.31), channel_id=1, source_target_pairs={{0,8},{4,12},{8,0},{12,4},{1,9},{5,13},{9,1},{13,5},{2,10},{6,14},... | collective-permute-start | bytes 165896 | tf_op jit(solution)/shard_map/ppermute | solution.py:252
  208.1 10.7 %collective-permute-start.11 = (bf16[24,1152]{1,0:T(8,128)(2,1)S(1)}, bf16[24,1152]{1,0:T(8,128)(2,1)S(1)}, u32[]{:S(2)}, u32[]{:S(2)}) collective-permute-start(bf16[24,1152]{1,0:T(8,128)(2,1)S(1)} %get-tuple-element.32), channel_id=1, source_target_pairs={{0,12},{4,0},{8,4},{12,8},{1,13},{5,1},{9,5},{13,9},{2,14},{6,2},{... | collective-permute-start | bytes 165896 | tf_op jit(solution)/shard_map/ppermute | solution.py:252

commit v3 on v2

--- a/solution.py
+++ b/solution.py
@@ -29,7 +29,7 @@
     return jax.ShapeDtypeStruct(dims, dtype)
 
 
-def call(body, outs, *args, scratch=(), flops=0):
+def call(body, outs, *args, scratch=(), flops=0, grant=VMEM_GRANT):
     size = sum(a.size * a.dtype.itemsize for a in args)
     size += sum(o.size * o.dtype.itemsize for o in outs)
     near = pl.BlockSpec(memory_space=pltpu.VMEM)
@@ -39,7 +39,7 @@
         in_specs=[near] * len(args),
         out_specs=tuple([near] * len(outs)),
         scratch_shapes=list(scratch),
-        compiler_params=pltpu.CompilerParams(vmem_limit_bytes=VMEM_GRANT),
+        compiler_params=pltpu.CompilerParams(vmem_limit_bytes=grant),
         cost_estimate=pl.CostEstimate(flops=flops, bytes_accessed=size, transcendentals=0),
     )(*args)
 
@@ -74,7 +74,7 @@
 
 def text_in(hidden_ref, gain_ref, out_ref):
     normed, _ = norm_parts(hidden_ref[...].astype(F32))
-    rows = (normed * gain_ref[...]).astype(BF16)
+    rows = (normed * gain_ref[...].reshape(1, -1)).astype(BF16)
     for k in range(out_ref.shape[0]):
         out_ref[k] = rows
 
@@ -99,22 +99,10 @@
     out_ref[:, width:] = (low + high).astype(F32).astype(BF16)
 
 
-def image_column(p0, p1, p2, p3, out_ref):
-    at = lax.axis_index("zh")
-    for k, piece in enumerate((p0, p1, p2, p3)):
-        out_ref[lax.rem(at + 4 - k, 4)] = piece[...]
-
-
-def image_all(q0, q1, q2, q3, teacher_ref, id_ref, image_ref, target_ref, tags):
-    at = lax.axis_index("x")
-    width = image_ref.shape[2]
-    rows = image_ref.shape[1]
-    for k, piece in enumerate((q0, q1, q2, q3)):
-        x = lax.rem(at + 4 - k, 4)
-        for z in range(4):
-            image_ref[z * 4 + x] = piece[z, :, :width]
-            tags[z * 4 + x] = piece[z, :, width:].astype(F32)
-    marks = tags[...].reshape(16 * rows, LANES).astype(BF16)
+def targets(image_ref, teacher_ref, id_ref, target_ref):
+    sides, _, rows, deep = image_ref.shape
+    group = sides * sides * rows
+    marks = image_ref[:, :, :, deep - LANES :].reshape(group, LANES)
     row = lax.broadcasted_iota(jnp.int32, (8, LANES), 0)
     lane = lax.broadcasted_iota(jnp.int32, (8, LANES), 1)
     pick = jnp.where(row == lane, 1.0, 0.0).astype(BF16)
@@ -122,7 +110,13 @@
     image_id = ids[0:1] + 128.0 * ids[1:2]
     text_id = column_of(id_ref).astype(F32)
     same = jnp.where(text_id == image_id, 0.5, 0.0)
-    target_ref[...] = same + 0.5 * jax.nn.sigmoid(teacher_ref[...].astype(F32))
+    down = lax.broadcasted_iota(jnp.int32, (group, group), 0)
+    along = lax.broadcasted_iota(jnp.int32, (1, group), 1)
+    block = along // rows
+    wanted = (lax.rem(block, sides) * sides + block // sides) * rows + lax.rem(along, rows)
+    order = jnp.where(down == wanted, 1.0, 0.0).astype(BF16)
+    teacher = dot(teacher_ref[...], order, NN)
+    target_ref[...] = same + 0.5 * jax.nn.sigmoid(teacher)
 
 
 def forward(rows_ref, w_in_ref, w_out_ref, part_ref, act_ref, slope_ref):
@@ -141,12 +135,12 @@
     for k in range(1, blocks):
         total = total + part_ref[k].astype(F32)
     residual = hidden_ref[...].astype(F32) + total
-    gain = gain_ref[...]
+    gain = gain_ref[...].reshape(1, width)
     normed, inverse = norm_parts(residual)
     final = normed * gain
     length = jnp.sqrt(jnp.sum(final * final, axis=-1, keepdims=True) + epsilon)
     unit = final / length
-    images = image_ref[...].reshape(blocks * rows, width)
+    images = image_ref[:, :, :, :width].reshape(blocks * rows, width)
     logits = dot(unit.astype(BF16), images, NT) * logit_scale + logit_bias
     pair_grad = (jax.nn.sigmoid(logits) - target_ref[...]).astype(BF16)
     text_grad = logit_scale * dot(pair_grad, images, NN)
@@ -244,7 +238,7 @@
 def last(keep_ref, g1, g2, g3, hidden_ref, gain_ref, grad_ref, out_ref):
     total = keep_ref[...] + g1[...].astype(F32) + g2[...].astype(F32) + g3[...].astype(F32)
     normed, inverse = norm_parts(hidden_ref[...].astype(F32))
-    out_ref[...] = grad_ref[...] + norm_backward(total * gain_ref[...], normed, inverse)
+    out_ref[...] = grad_ref[...] + norm_backward(total * gain_ref[...].reshape(1, -1), normed, inverse)
 
 
 def shift(value, axis, by):
@@ -260,8 +254,6 @@
     blocks = lax.axis_size(BLK)
     ring = lax.axis_size(RING)
     group = rows * blocks
-    gain_mlp = gain_mlp.reshape(1, width)
-    gain_final = gain_final.reshape(1, width)
     ids = pair_ids.reshape(1, rows)
     w_in_rows = w_in.T
     teacher = teacher_logits[0].T
@@ -272,18 +264,7 @@
     group_input = lax.all_to_all(copies, BLK, 0, 0)
 
     (payload,) = call(image_in, [shape((rows, width + LANES), BF16)], image_embeds, ids)
-    near = [shift(payload, "zh", k) for k in (1, 2, 3)]
-    (column,) = call(image_column, [shape((4, rows, width + LANES), BF16)], payload, *near)
-    far = [shift(column, "x", k) for k in (1, 2, 3)]
-    images, target = call(
-        image_all,
-        [spread, shape((rows, group), F32)],
-        column,
-        *far,
-        teacher,
-        ids,
-        scratch=[pltpu.VMEM((blocks, rows, LANES), F32)],
-    )
+    column = lax.all_gather(payload, "zh")
 
     part, act, slope = call(
         forward,
@@ -293,6 +274,9 @@
         w_out,
         flops=2 * matmul,
     )
+    part, column = lax.optimization_barrier((part, column))
+    images = lax.all_gather(column, "x")
+    (target,) = call(targets, [shape((rows, group), F32)], images, teacher, ids)
     parts = lax.all_to_all(part, BLK, 0, 0)
     copies, grad_residual = call(
         middle, [spread, shape((rows, width), F32)], parts, hidden_in, gain_final, images, target

time: 222 us -> 211 us (0.950)
  blocking collectives: 114 us -> 127 us
  starting transfers between devices: 67.7 us -> 54.8 us
  waiting for transfers between devices: 24.3 us -> 12.3 us
    all_gather x0 -> x2, blocking collectives: none -> 49.3 us  [the longest x1 29.5 us: per_device(): column = lax.all_gather(payload, 'zh')]
    all_to_all x1 -> x0, blocking collectives: 33.2 us -> none  [per_device(): group_input = lax.all_to_all(copies, BLK, 0, 0)]
    ppermute x14 -> x8, starting transfers between devices: 61.3 us -> 34.3 us  [shift(): lax.ppermute(value, axis, [(i, (i + by) % length) for i in range(length)])]
    all_to_all x0 -> x1, starting transfers between devices: none -> 13.5 us  [per_device(): group_input = lax.all_to_all(copies, BLK, 0, 0)]
    ppermute x14 -> x8, waiting for transfers between devices: 24.3 us -> 12.3 us  [shift(): lax.ppermute(value, axis, [(i, (i + by) % length) for i in range(length)])]
    all_to_all x1, blocking collectives: 36.6 us -> 28.8 us  [per_device(): slices = lax.all_to_all(mine, RING, 0, 0)]
    all_to_all x1, blocking collectives: 21 us -> 25.5 us  [per_device(): group_grads = lax.all_to_all(copies, BLK, 0, 0)]
    pallas_call x15 -> x14, Pallas kernels: 9.54 us -> 11.3 us  [call(): pl.pallas_call(body, out_shape=tuple(outs), in_specs=[near] * len(args),...]
  transfers between devices with their start and end apart: 15 -> 10, of which waited for: 10 -> 5; matrix products, arithmetic and copies ran while one was open for 0% -> 0% of each run, Pallas kernels for 1% -> 1%
where the time goes in v3:
time: 211 us; the launch traced here: 209 us
  blocking collectives  127 us (60%)
  starting transfers between devices  54.8 us (26%)
  waiting for transfers between devices  12.3 us (6%)
  Pallas kernels  11.3 us (5%)
  local copies, waits for them, and re-layouts  3.37 us (2%)
    ppermute x8, starting transfers between devices, shift(): lax.ppermute(value, axis, [(i, (i + by) % length) for i in range(length)])  34.3 us
    all_gather x1, blocking collectives, per_device(): column = lax.all_gather(payload, 'zh')  29.5 us
    all_to_all x1, blocking collectives, per_device(): slices = lax.all_to_all(mine, RING, 0, 0)  28.8 us
    all_to_all x1, blocking collectives, per_device(): group_grads = lax.all_to_all(copies, BLK, 0, 0)  25.5 us
    all_to_all x1, blocking collectives, per_device(): whole = lax.all_to_all(copies, RING, 0, 0).reshape(tall, LANES)  22.9 us
    all_gather x1, blocking collectives, per_device(): images = lax.all_gather(column, 'x')  19.8 us
    all_to_all x1, starting transfers between devices, per_device(): group_input = lax.all_to_all(copies, BLK, 0, 0)  13.5 us
    ppermute x8, waiting for transfers between devices, shift(): lax.ppermute(value, axis, [(i, (i + by) % length) for i in range(length)])  12.3 us
  transfers between devices with their start and end apart: 10, of which 5 were waited for; matrix products, arithmetic and copies ran while one was open for 0% of the time, Pallas kernels for 1%

profile of v3, /device:TPU:1, one launch (start us, length us, event | category | flops | bytes accessed | tf_op | source)
XLA Modules:
  0.0 209.2 jit_solution(7741938396662351821)
XLA Ops:
  0.6 0.8 copy-done.7
  1.4 0.7 copy-done.10
  2.1 1.2 shard_map.103
  3.3 13.5 %all-to-all-start = ((bf16[16,24,1152]{2,1,0:T(8,128)(2,1)}), bf16[16,24,1152]{2,1,0:T(8,128)(2,1)S(1)}, u32[]{:S(2)}, u32[]{:S(2)}) async-start(bf16[16,24,1152]{2,1,0:T(8,128)(2,1)} %shard_map.103), calls=%async_computation | async-start | bytes 1769472 | tf_op jit(solution)/shard_map/all_to_all | solution.py:264
  17.0 29.5 %all-gather = bf16[96,1280]{1,0:T(8,128)(2,1)} all-gather(bf16[24,1280]{1,0:T(8,128)(2,1)S(1)} %shard_map.105), channel_id=2, replica_groups=mesh['zl'=2,'y'=8,'co'=2,'zh'=4,'x'=4] {'zh'}, dimensions={0}, use_global_device_ids=true | all-gather | bytes 307200 | tf_op jit(solution)/shard_map/all_gather | solution.py:267
  46.5 2.4 %shard_map.104 = (bf16[16,24,1152]{2,1,0:T(8,128)(2,1)}, bf16[384,269]{1,0:T(8,128)(2,1)S(1)}, f32[384,269]{1,0:T(8,128)S(1)}) custom-call(bf16[16,24,1152]{2,1,0:T(8,128)(2,1)S(1)} %all-to-all-done.rows_ref.refs_3_, bf16[269,1152]{1,0:T(8,128)(2,1)S(1)} %bitcast.13, bf16[269,1152]{1,0:T(8,128)(2,1)S(1)} %copy-done), custom_call_target="tpu_custom_call" | custom-call | flops 475987968 | bytes 3628800 | tf_op jit(solution)/shard_map/pallas_call | solution.py:36
  48.9 0.7 copy-done.3
  49.6 0.8 copy-done.5
  50.4 7.0 %all-to-all-start.1 = ((bf16[16,24,1152]{2,1,0:T(8,128)(2,1)}), bf16[16,24,1152]{2,1,0:T(8,128)(2,1)S(1)}, u32[]{:S(2)}, u32[]{:S(2)}) async-start(bf16[16,24,1152]{2,1,0:T(8,128)(2,1)} %get-tuple-element.21), calls=%async_computation.1 | async-start | bytes 1769472 | tf_op jit(solution)/shard_map/all_to_all | solution.py:280
  57.4 19.8 %all-gather.1 = bf16[16,24,1280]{2,1,0:T(8,128)(2,1)S(1)} all-gather(bf16[4,24,1280]{2,1,0:T(8,128)(2,1)} %bitcast.18), channel_id=3, replica_groups=mesh['zl'=2,'y'=8,'co'=2,'zh'=4,'x'=4] {'x'}, dimensions={0}, use_global_device_ids=true | all-gather | bytes 1228800 | tf_op jit(solution)/shard_map/all_gather | solution.py:278
  77.5 1.3 shard_map.107
  78.8 25.5 %all_to_all.25.rows_ref.refs_1_ = bf16[16,24,1152]{2,1,0:T(8,128)(2,1)S(1)} all-to-all(bf16[16,24,1152]{2,1,0:T(8,128)(2,1)S(1)} %get-tuple-element.23), channel_id=1, replica_groups=mesh['zl'=2,'y'=8,'co'=2,'zh'=4,'x'=4] {'zh','x'}, dimensions={0} | all-to-all | bytes 1769472 | tf_op jit(solution)/shard_map/all_to_all | solution.py:284
  104.3 0.7 shard_map.108.grad_ref.refs_2_
  105.3 0.9 shard_map.113
  106.2 8.4 %collective-permute-start.6 = (bf16[2560,128]{1,0:T(8,128)(2,1)S(1)}, bf16[2560,128]{1,0:T(8,128)(2,1)S(1)}, u32[]{:S(2)}, u32[]{:S(2)}) collective-permute-start(bf16[2560,128]{1,0:T(8,128)(2,1)S(1)} %shard_map.113), channel_id=1, source_target_pairs={{0,16},{16,0},{1,17},{17,1},{2,18},{18,2},{3,19},{19,3},{4,20},{20... | collective-permute-start | bytes 1966088 | tf_op jit(solution)/shard_map/ppermute | solution.py:246
  114.6 0.9 shard_map.112.kept_ref
  115.5 0.8 collective-permute-done.6.got_ref
  116.4 28.8 %all_to_all.26.slices_ref = bf16[16,160,128]{2,1,0:T(8,128)(2,1)S(1)} all-to-all(bf16[16,160,128]{2,1,0:T(8,128)(2,1)S(1)} %shard_map.114), channel_id=1, replica_groups=mesh['zl'=2,'y'=8,'co'=2,'zh'=4,'x'=4] {'zl','y'}, dimensions={0} | all-to-all | bytes 1310720 | tf_op jit(solution)/shard_map/all_to_all | solution.py:308
  145.3 22.9 %all_to_all.27 = bf16[16,160,128]{2,1,0:T(8,128)(2,1)S(1)} all-to-all(bf16[16,160,128]{2,1,0:T(8,128)(2,1)S(1)} %shard_map.115), channel_id=1, replica_groups=mesh['zl'=2,'y'=8,'co'=2,'zh'=4,'x'=4] {'zl','y'}, dimensions={0} | all-to-all | bytes 1310720 | tf_op jit(solution)/shard_map/all_to_all | solution.py:333
  168.2 5.4 %collective-permute-start.7 = (bf16[2560,128]{1,0:T(8,128)(2,1)S(1)}, bf16[2560,128]{1,0:T(8,128)(2,1)S(1)}, u32[]{:S(2)}, u32[]{:S(2)}) collective-permute-start(bf16[2560,128]{1,0:T(8,128)(2,1)S(1)} %bitcast.11), channel_id=1, source_target_pairs={{0,16},{16,0},{1,17},{17,1},{2,18},{18,2},{3,19},{19,3},{4,20},{20... | collective-permute-start | bytes 1966088 | tf_op jit(solution)/shard_map/ppermute | solution.py:246
  173.7 0.7 shard_map.109
  174.4 1.9 collective-permute-start
  176.4 3.9 %collective-permute-start.1 = (bf16[4,24,1152]{2,1,0:T(8,128)(2,1)S(1)}, bf16[4,24,1152]{2,1,0:T(8,128)(2,1)S(1)}, u32[]{:S(2)}, u32[]{:S(2)}) collective-permute-start(bf16[4,24,1152]{2,1,0:T(8,128)(2,1)S(1)} %get-tuple-element.27), channel_id=1, source_target_pairs={{0,2},{1,3},{2,0},{3,1},{4,6},{5,7},{6,4},{7,5},{8,10},{9,11},{10,... | collective-permute-start | bytes 663560 | tf_op jit(solution)/shard_map/ppermute | solution.py:246
  180.3 3.3 %collective-permute-start.2 = (bf16[4,24,1152]{2,1,0:T(8,128)(2,1)S(1)}, bf16[4,24,1152]{2,1,0:T(8,128)(2,1)S(1)}, u32[]{:S(2)}, u32[]{:S(2)}) collective-permute-start(bf16[4,24,1152]{2,1,0:T(8,128)(2,1)S(1)} %get-tuple-element.28), channel_id=1, source_target_pairs={{0,3},{1,0},{2,1},{3,2},{4,7},{5,4},{6,5},{7,6},{8,11},{9,8},{10,9... | collective-permute-start | bytes 663560 | tf_op jit(solution)/shard_map/ppermute | solution.py:246
  183.6 5.6 %collective-permute-done.k1 = bf16[4,24,1152]{2,1,0:T(8,128)(2,1)S(1)} collective-permute-done((bf16[4,24,1152]{2,1,0:T(8,128)(2,1)S(1)}, bf16[4,24,1152]{2,1,0:T(8,128)(2,1)S(1)}, u32[]{:S(2)}, u32[]{:S(2)}) %collective-permute-start) | collective-permute-done | bytes 221216 | tf_op jit(solution)/shard_map/ppermute | solution.py:246
  189.2 2.2 %collective-permute-done.2.k3 = bf16[4,24,1152]{2,1,0:T(8,128)(2,1)S(1)} collective-permute-done((bf16[4,24,1152]{2,1,0:T(8,128)(2,1)S(1)}, bf16[4,24,1152]{2,1,0:T(8,128)(2,1)S(1)}, u32[]{:S(2)}, u32[]{:S(2)}) %collective-permute-start.2) | collective-permute-done | bytes 221216 | tf_op jit(solution)/shard_map/ppermute | solution.py:246
  191.6 2.6 %collective-permute-start.3 = (bf16[24,1152]{1,0:T(8,128)(2,1)S(1)}, bf16[24,1152]{1,0:T(8,128)(2,1)S(1)}, u32[]{:S(2)}, u32[]{:S(2)}) collective-permute-start(bf16[24,1152]{1,0:T(8,128)(2,1)S(1)} %get-tuple-element.30), channel_id=1, source_target_pairs={{0,4},{4,8},{8,12},{12,0},{1,5},{5,9},{9,13},{13,1},{2,6},{6,10},{... | collective-permute-start | bytes 165896 | tf_op jit(solution)/shard_map/ppermute | solution.py:246
  194.3 5.3 %collective-permute-start.4 = (bf16[24,1152]{1,0:T(8,128)(2,1)S(1)}, bf16[24,1152]{1,0:T(8,128)(2,1)S(1)}, u32[]{:S(2)}, u32[]{:S(2)}) collective-permute-start(bf16[24,1152]{1,0:T(8,128)(2,1)S(1)} %get-tuple-element.31), channel_id=1, source_target_pairs={{0,8},{4,12},{8,0},{12,4},{1,9},{5,13},{9,1},{13,5},{2,10},{6,14},... | collective-permute-start | bytes 165896 | tf_op jit(solution)/shard_map/ppermute | solution.py:246
  199.6 3.4 %collective-permute-start.5 = (bf16[24,1152]{1,0:T(8,128)(2,1)S(1)}, bf16[24,1152]{1,0:T(8,128)(2,1)S(1)}, u32[]{:S(2)}, u32[]{:S(2)}) collective-permute-start(bf16[24,1152]{1,0:T(8,128)(2,1)S(1)} %get-tuple-element.32), channel_id=1, source_target_pairs={{0,12},{4,0},{8,4},{12,8},{1,13},{5,1},{9,5},{13,9},{2,14},{6,2},{... | collective-permute-start | bytes 165896 | tf_op jit(solution)/shard_map/ppermute | solution.py:246
  203.2 3.5 %collective-permute-done.5.g3 = bf16[24,1152]{1,0:T(8,128)(2,1)S(1)} collective-permute-done((bf16[24,1152]{1,0:T(8,128)(2,1)S(1)}, bf16[24,1152]{1,0:T(8,128)(2,1)S(1)}, u32[]{:S(2)}, u32[]{:S(2)}) %collective-permute-start.5) | collective-permute-done | bytes 55328 | tf_op jit(solution)/shard_map/ppermute | solution.py:246
  206.7 0.9 shard_map.111
  207.6 1.6 shard_map.116
  (37 shorter events, 1.3 us)
Async XLA Ops:
  0.6 0.8 copy-start.7
  1.4 0.7 copy-start.10
  2.1 14.7 %copy-start.9 = (bf16[24,1152]{1,0:T(8,128)(2,1)S(1)}, bf16[24,1152]{1,0:T(8,128)(2,1)}, u32[]{:S(2)}) copy-start(bf16[24,1152]{1,0:T(8,128)(2,1)} %image_ref.1) | copy-start | bytes 165892
  2.1 14.7 %copy-start.14 = (s32[24]{0:T(128)S(1)}, s32[24]{0:T(128)}, u32[]{:S(2)}) copy-start(s32[24]{0:T(128)} %param.14) | copy-start | bytes 292
  3.3 43.2 %copy-start = (bf16[269,1152]{1,0:T(8,128)(2,1)S(1)}, bf16[269,1152]{1,0:T(8,128)(2,1)}, u32[]{:S(2)}) copy-start(bf16[269,1152]{1,0:T(8,128)(2,1)} %w_out_ref.3) | copy-start | bytes 1859332
  3.3 43.2 %copy-start.1 = (bf16[1152,269]{0,1:T(8,128)(2,1)S(1)}, bf16[1152,269]{0,1:T(8,128)(2,1)}, u32[]{:S(2)}) copy-start(bf16[1152,269]{0,1:T(8,128)(2,1)} %param.11) | copy-start | bytes 1859332
  3.3 43.2 %all-to-all-start = ((bf16[16,24,1152]{2,1,0:T(8,128)(2,1)}), bf16[16,24,1152]{2,1,0:T(8,128)(2,1)S(1)}, u32[]{:S(2)}, u32[]{:S(2)}) async-start(bf16[16,24,1152]{2,1,0:T(8,128)(2,1)} %shard_map.103), calls=%async_computation | async-start | bytes 1769472 | tf_op jit(solution)/shard_map/all_to_all | solution.py:264
  48.9 0.7 copy-start.3
  49.6 0.8 copy-start.5
  50.4 26.8 %copy-start.12 = (bf16[1,384,24]{1,2,0:T(8,128)(2,1)S(1)}, bf16[1,384,24]{1,2,0:T(8,128)(2,1)}, u32[]{:S(2)}) copy-start(bf16[1,384,24]{1,2,0:T(8,128)(2,1)} %param.15) | copy-start | bytes 55300
  50.4 27.1 %all-to-all-start.1 = ((bf16[16,24,1152]{2,1,0:T(8,128)(2,1)}), bf16[16,24,1152]{2,1,0:T(8,128)(2,1)S(1)}, u32[]{:S(2)}, u32[]{:S(2)}) async-start(bf16[16,24,1152]{2,1,0:T(8,128)(2,1)} %get-tuple-element.21), calls=%async_computation.1 | async-start | bytes 1769472 | tf_op jit(solution)/shard_map/all_to_all | solution.py:280
  57.4 20.1 %copy-start.8 = (bf16[24,1152]{1,0:T(8,128)(2,1)S(1)}, bf16[24,1152]{1,0:T(8,128)(2,1)}, u32[]{:S(2)}) copy-start(bf16[24,1152]{1,0:T(8,128)(2,1)} %hidden_ref.5) | copy-start | bytes 165892
  57.4 20.1 %copy-start.13 = (f32[1152]{0:T(1024)S(1)}, f32[1152]{0:T(1024)}, u32[]{:S(2)}) copy-start(f32[1152]{0:T(1024)} %gain_ref.4) | copy-start | bytes 13828
  78.7 25.5 %copy-start.6 = (f32[384,269]{1,0:T(8,128)S(1)}, f32[384,269]{1,0:T(8,128)}, u32[]{:S(2)}) copy-start(f32[384,269]{1,0:T(8,128)} %copy-done.5) | copy-start | bytes 1239556
  104.3 1.0 copy-start.4
  106.2 10.1 %collective-permute-start.6 = (bf16[2560,128]{1,0:T(8,128)(2,1)S(1)}, bf16[2560,128]{1,0:T(8,128)(2,1)S(1)}, u32[]{:S(2)}, u32[]{:S(2)}) collective-permute-start(bf16[2560,128]{1,0:T(8,128)(2,1)S(1)} %shard_map.113), channel_id=1, source_target_pairs={{0,16},{16,0},{1,17},{17,1},{2,18},{18,2},{3,19},{19,3},{4,20},{20... | collective-permute-start | bytes 1966088 | tf_op jit(solution)/shard_map/ppermute | solution.py:246
  145.2 28.5 %copy-start.2 = (bf16[1152,269]{0,1:T(8,128)(2,1)S(1)}, bf16[1152,269]{0,1:T(8,128)(2,1)}, u32[]{:S(2)}) copy-start(bf16[1152,269]{0,1:T(8,128)(2,1)} %param.11) | copy-start | bytes 1859332
  145.3 61.4 %copy-start.11 = (f32[1152]{0:T(1024)S(1)}, f32[1152]{0:T(1024)}, u32[]{:S(2)}) copy-start(f32[1152]{0:T(1024)} %gain_ref.5) | copy-start | bytes 13828
  168.2 39.4 %collective-permute-start.7 = (bf16[2560,128]{1,0:T(8,128)(2,1)S(1)}, bf16[2560,128]{1,0:T(8,128)(2,1)S(1)}, u32[]{:S(2)}, u32[]{:S(2)}) collective-permute-start(bf16[2560,128]{1,0:T(8,128)(2,1)S(1)} %bitcast.11), channel_id=1, source_target_pairs={{0,16},{16,0},{1,17},{17,1},{2,18},{18,2},{3,19},{19,3},{4,20},{20... | collective-permute-start | bytes 1966088 | tf_op jit(solution)/shard_map/ppermute | solution.py:246
  174.4 14.8 %collective-permute-start = (bf16[4,24,1152]{2,1,0:T(8,128)(2,1)S(1)}, bf16[4,24,1152]{2,1,0:T(8,128)(2,1)S(1)}, u32[]{:S(2)}, u32[]{:S(2)}) collective-permute-start(bf16[4,24,1152]{2,1,0:T(8,128)(2,1)S(1)} %get-tuple-element.26), channel_id=1, source_target_pairs={{0,1},{1,2},{2,3},{3,0},{4,5},{5,6},{6,7},{7,4},{8,9},{9,10},{10,1... | collective-permute-start | bytes 663560 | tf_op jit(solution)/shard_map/ppermute | solution.py:246
  176.4 12.9 %collective-permute-start.1 = (bf16[4,24,1152]{2,1,0:T(8,128)(2,1)S(1)}, bf16[4,24,1152]{2,1,0:T(8,128)(2,1)S(1)}, u32[]{:S(2)}, u32[]{:S(2)}) collective-permute-start(bf16[4,24,1152]{2,1,0:T(8,128)(2,1)S(1)} %get-tuple-element.27), channel_id=1, source_target_pairs={{0,2},{1,3},{2,0},{3,1},{4,6},{5,7},{6,4},{7,5},{8,10},{9,11},{10,... | collective-permute-start | bytes 663560 | tf_op jit(solution)/shard_map/ppermute | solution.py:246
  180.3 11.1 %collective-permute-start.2 = (bf16[4,24,1152]{2,1,0:T(8,128)(2,1)S(1)}, bf16[4,24,1152]{2,1,0:T(8,128)(2,1)S(1)}, u32[]{:S(2)}, u32[]{:S(2)}) collective-permute-start(bf16[4,24,1152]{2,1,0:T(8,128)(2,1)S(1)} %get-tuple-element.28), channel_id=1, source_target_pairs={{0,3},{1,0},{2,1},{3,2},{4,7},{5,4},{6,5},{7,6},{8,11},{9,8},{10,9... | collective-permute-start | bytes 663560 | tf_op jit(solution)/shard_map/ppermute | solution.py:246
  191.6 11.4 %collective-permute-start.3 = (bf16[24,1152]{1,0:T(8,128)(2,1)S(1)}, bf16[24,1152]{1,0:T(8,128)(2,1)S(1)}, u32[]{:S(2)}, u32[]{:S(2)}) collective-permute-start(bf16[24,1152]{1,0:T(8,128)(2,1)S(1)} %get-tuple-element.30), channel_id=1, source_target_pairs={{0,4},{4,8},{8,12},{12,0},{1,5},{5,9},{9,13},{13,1},{2,6},{6,10},{... | collective-permute-start | bytes 165896 | tf_op jit(solution)/shard_map/ppermute | solution.py:246
  194.3 8.9 %collective-permute-start.4 = (bf16[24,1152]{1,0:T(8,128)(2,1)S(1)}, bf16[24,1152]{1,0:T(8,128)(2,1)S(1)}, u32[]{:S(2)}, u32[]{:S(2)}) collective-permute-start(bf16[24,1152]{1,0:T(8,128)(2,1)S(1)} %get-tuple-element.31), channel_id=1, source_target_pairs={{0,8},{4,12},{8,0},{12,4},{1,9},{5,13},{9,1},{13,5},{2,10},{6,14},... | collective-permute-start | bytes 165896 | tf_op jit(solution)/shard_map/ppermute | solution.py:246
  199.6 7.1 %collective-permute-start.5 = (bf16[24,1152]{1,0:T(8,128)(2,1)S(1)}, bf16[24,1152]{1,0:T(8,128)(2,1)S(1)}, u32[]{:S(2)}, u32[]{:S(2)}) collective-permute-start(bf16[24,1152]{1,0:T(8,128)(2,1)S(1)} %get-tuple-element.32), channel_id=1, source_target_pairs={{0,12},{4,0},{8,4},{12,8},{1,13},{5,1},{9,5},{13,9},{2,14},{6,2},{... | collective-permute-start | bytes 165896 | tf_op jit(solution)/shard_map/ppermute | solution.py:246

commit v4 on v3

--- a/solution.py
+++ b/solution.py
@@ -17,6 +17,7 @@
 RING = ("zl", "y")
 LANES = 128
 VMEM_GRANT = 8 * 2**20
+WHOLE_GRANT = 60 * 2**20
 F32 = jnp.float32
 BF16 = jnp.bfloat16
 
@@ -29,14 +30,15 @@
     return jax.ShapeDtypeStruct(dims, dtype)
 
 
-def call(body, outs, *args, scratch=(), flops=0, grant=VMEM_GRANT):
+def call(body, outs, *args, far_in=(), scratch=(), flops=0, grant=VMEM_GRANT):
     size = sum(a.size * a.dtype.itemsize for a in args)
     size += sum(o.size * o.dtype.itemsize for o in outs)
     near = pl.BlockSpec(memory_space=pltpu.VMEM)
+    far = pl.BlockSpec(memory_space=pl.ANY)
     return pl.pallas_call(
         body,
         out_shape=tuple(outs),
-        in_specs=[near] * len(args),
+        in_specs=[far if k in far_in else near for k in range(len(args))],
         out_specs=tuple([near] * len(outs)),
         scratch_shapes=list(scratch),
         compiler_params=pltpu.CompilerParams(vmem_limit_bytes=grant),
@@ -72,13 +74,6 @@
     return gelu_value, gelu_slope
 
 
-def text_in(hidden_ref, gain_ref, out_ref):
-    normed, _ = norm_parts(hidden_ref[...].astype(F32))
-    rows = (normed * gain_ref[...].reshape(1, -1)).astype(BF16)
-    for k in range(out_ref.shape[0]):
-        out_ref[k] = rows
-
-
 def column_of(row_ref):
     count = row_ref.shape[1]
     spread = jnp.broadcast_to(row_ref[...], (count, count))
@@ -87,16 +82,32 @@
     return jnp.sum(jnp.where(down == along, spread, 0), axis=1, keepdims=True)
 
 
-def image_in(image_ref, id_ref, out_ref):
+def prepare(
+    hidden_hbm, gain_hbm, image_hbm, id_hbm, out_ref, hidden_ref, gain_ref, image_ref, id_ref, sems
+):
+    width = hidden_ref.shape[1]
+    arrays = ((hidden_hbm, hidden_ref), (gain_hbm, gain_ref), (image_hbm, image_ref), (id_hbm, id_ref))
+    moves = [pltpu.make_async_copy(src, dst, sems.at[k]) for k, (src, dst) in enumerate(arrays)]
+    for move in moves:
+        move.start()
+    for move in moves:
+        move.wait()
+    normed, _ = norm_parts(hidden_ref[...].astype(F32))
+    out_ref[:, :width] = (normed * gain_ref[...].reshape(1, width)).astype(BF16)
     image = image_ref[...].astype(F32)
-    width = image.shape[1]
     scale = lax.rsqrt(jnp.sum(image * image, axis=-1, keepdims=True) + epsilon)
-    out_ref[:, :width] = (image * scale).astype(BF16)
+    out_ref[:, width : 2 * width] = (image * scale).astype(BF16)
     ids = column_of(id_ref)
     lane = lax.broadcasted_iota(jnp.int32, (image.shape[0], LANES), 1)
     low = jnp.where(lane == 0, ids & 127, 0)
     high = jnp.where(lane == 1, ids >> 7, 0)
-    out_ref[:, width:] = (low + high).astype(F32).astype(BF16)
+    out_ref[:, 2 * width :] = (low + high).astype(F32).astype(BF16)
+
+
+def split(both_ref, rows_ref, image_ref):
+    width = rows_ref.shape[2]
+    rows_ref[...] = both_ref[:, :, :width]
+    image_ref[...] = both_ref[:, :, width:]
 
 
 def targets(image_ref, teacher_ref, id_ref, target_ref):
@@ -119,8 +130,11 @@
     target_ref[...] = same + 0.5 * jax.nn.sigmoid(teacher)
 
 
-def forward(rows_ref, w_in_ref, w_out_ref, part_ref, act_ref, slope_ref):
+def forward(all_ref, w_in_ref, w_out_ref, part_ref, act_ref, slope_ref, rows_ref):
     blocks, rows, width = part_ref.shape
+    for x in range(4):
+        for z in range(4):
+            rows_ref[z * 4 + x] = all_ref[x, z]
     pre_act = dot(rows_ref[...].reshape(blocks * rows, width), w_in_ref[...], NT)
     value, slope = gelu_both(pre_act)
     act = value.astype(BF16)
@@ -260,16 +274,32 @@
     spread = shape((blocks, rows, width), BF16)
     matmul = 2 * group * units * width
 
-    (copies,) = call(text_in, [spread], hidden_in, gain_mlp)
-    group_input = lax.all_to_all(copies, BLK, 0, 0)
-
-    (payload,) = call(image_in, [shape((rows, width + LANES), BF16)], image_embeds, ids)
-    column = lax.all_gather(payload, "zh")
-
-    part, act, slope = call(
+    (own_rows,) = call(
+        prepare,
+        [shape((rows, 2 * width + LANES), BF16)],
+        hidden_in,
+        gain_mlp,
+        image_embeds,
+        ids,
+        far_in=(0, 1, 2, 3),
+        scratch=[
+            pltpu.VMEM(hidden_in.shape, BF16),
+            pltpu.VMEM(gain_mlp.shape, F32),
+            pltpu.VMEM(image_embeds.shape, BF16),
+            pltpu.VMEM(ids.shape, ids.dtype),
+            pltpu.SemaphoreType.DMA((4,)),
+        ],
+        grant=WHOLE_GRANT,
+    )
+    both = lax.all_gather(own_rows, "zh")
+    rows_column, column = call(
+        split, [shape((4, rows, width), BF16), shape((4, rows, width + LANES), BF16)], both
+    )
+    everything = lax.all_gather(rows_column, "x")
+    part, act, slope, group_input = call(
         forward,
-        [spread, shape((group, units), BF16), shape((group, units), F32)],
-        group_input,
+        [spread, shape((group, units), BF16), shape((group, units), F32), spread],
+        everything,
         w_in_rows,
         w_out,
         flops=2 * matmul,

time: 211 us -> 197 us (0.934)
  starting transfers between devices: 54.8 us -> 47.2 us
  blocking collectives: 127 us -> 121 us
    all_to_all x1 -> x0, starting transfers between devices: 13.5 us -> none  [per_device(): group_input = lax.all_to_all(copies, BLK, 0, 0)]
    ppermute x8, starting transfers between devices: 34.3 us -> 40.5 us  [shift(): lax.ppermute(value, axis, [(i, (i + by) % length) for i in range(length)])]
    all_to_all x1, blocking collectives: 28.8 us -> 24.1 us  [per_device(): slices = lax.all_to_all(mine, RING, 0, 0)]
    all_gather x1, blocking collectives: 19.8 us -> 16.8 us  [per_device(): images = lax.all_gather(column, 'x')]
    all_gather x1 -> x2, blocking collectives: 29.5 us -> 31.9 us  [the longest x1 20.2 us: per_device(): both = lax.all_gather(own_rows, 'zh')]
  transfers between devices with their start and end apart: 10 -> 9, of which waited for: 5 -> 5; matrix products, arithmetic and copies ran while one was open for 0% -> 0% of each run, Pallas kernels for 1% -> 2%
where the time goes in v4:
time: 197 us; the launch traced here: 196 us
  blocking collectives  121 us (61%)
  starting transfers between devices  47.2 us (24%)
  waiting for transfers between devices  12.9 us (7%)
  Pallas kernels  11.9 us (6%)
    ppermute x8, starting transfers between devices, shift(): lax.ppermute(value, axis, [(i, (i + by) % length) for i in range(length)])  40.5 us
    all_to_all x1, blocking collectives, per_device(): group_grads = lax.all_to_all(copies, BLK, 0, 0)  25.2 us
    all_to_all x1, blocking collectives, per_device(): slices = lax.all_to_all(mine, RING, 0, 0)  24.1 us
    all_to_all x1, blocking collectives, per_device(): whole = lax.all_to_all(copies, RING, 0, 0).reshape(tall, LANES)  22.9 us
    all_gather x1, blocking collectives, per_device(): both = lax.all_gather(own_rows, 'zh')  20.2 us
    all_gather x1, blocking collectives, per_device(): images = lax.all_gather(column, 'x')  16.8 us
    ppermute x8, waiting for transfers between devices, shift(): lax.ppermute(value, axis, [(i, (i + by) % length) for i in range(length)])  12.9 us
    pallas_call x14, Pallas kernels, call(): pl.pallas_call(body, out_shape=tuple(outs), in_specs=[far if k in far_in...  11.9 us
  transfers between devices with their start and end apart: 9, of which 5 were waited for; matrix products, arithmetic and copies ran while one was open for 0% of the time, Pallas kernels for 2%

profile of v4, /device:TPU:1, one launch (start us, length us, event | category | flops | bytes accessed | tf_op | source)
XLA Modules:
  0.0 195.7 jit_solution(13444192235160413376)
XLA Ops:
  0.7 1.8 shard_map.103
  2.5 20.2 %all-gather = bf16[96,2432]{1,0:T(8,128)(2,1)S(1)} all-gather(bf16[24,2432]{1,0:T(8,128)(2,1)} %shard_map.103), channel_id=2, replica_groups=mesh['zl'=2,'y'=8,'co'=2,'zh'=4,'x'=4] {'zh'}, dimensions={0}, use_global_device_ids=true | all-gather | bytes 583680 | tf_op jit(solution)/shard_map/all_gather | solution.py:294
  22.7 11.8 %all-gather.1 = bf16[16,24,1152]{2,1,0:T(8,128)(2,1)S(1)} all-gather(bf16[4,24,1152]{2,1,0:T(8,128)(2,1)S(1)} %get-tuple-element.23), channel_id=3, replica_groups=mesh['zl'=2,'y'=8,'co'=2,'zh'=4,'x'=4] {'x'}, dimensions={0}, use_global_device_ids=true | all-gather | bytes 1105920 | tf_op jit(solution)/shard_map/all_gather | solution.py:298
  34.5 2.4 %shard_map.105 = (bf16[16,24,1152]{2,1,0:T(8,128)(2,1)}, bf16[384,269]{1,0:T(8,128)(2,1)S(1)}, f32[384,269]{1,0:T(8,128)S(1)}, bf16[16,24,1152]{2,1,0:T(8,128)(2,1)S(1)}) custom-call(bf16[4,4,24,1152]{3,2,1,0:T(8,128)(2,1)S(1)} %bitcast.12, bf16[269,1152]{1,0:T(8,128)(2,1)S(1)} %bitcast.15, bf16[269,1152]{1,0:T(8,128)(2,1)S(1)} %copy-done), custom_call_target="tpu_custom_call" | custom-call | flops 475987968 | bytes 4513536 | tf_op jit(solution)/shard_map/pallas_call | solution.py:38
  36.9 0.7 copy-done.3
  37.6 0.8 copy-done.5
  38.4 6.7 %all-to-all-start = ((bf16[16,24,1152]{2,1,0:T(8,128)(2,1)}), bf16[16,24,1152]{2,1,0:T(8,128)(2,1)S(1)}, u32[]{:S(2)}, u32[]{:S(2)}) async-start(bf16[16,24,1152]{2,1,0:T(8,128)(2,1)} %get-tuple-element.26), calls=%async_computation | async-start | bytes 1769472 | tf_op jit(solution)/shard_map/all_to_all | solution.py:310
  45.1 16.8 %all-gather.2 = bf16[16,24,1280]{2,1,0:T(8,128)(2,1)S(1)} all-gather(bf16[4,24,1280]{2,1,0:T(8,128)(2,1)} %copy-done.8), channel_id=4, replica_groups=mesh['zl'=2,'y'=8,'co'=2,'zh'=4,'x'=4] {'x'}, dimensions={0}, use_global_device_ids=true | all-gather | bytes 1228800 | tf_op jit(solution)/shard_map/all_gather | solution.py:308
  62.1 1.3 shard_map.107
  63.4 25.2 %all_to_all.20.rows_ref.refs_1_ = bf16[16,24,1152]{2,1,0:T(8,128)(2,1)S(1)} all-to-all(bf16[16,24,1152]{2,1,0:T(8,128)(2,1)S(1)} %get-tuple-element.28), channel_id=1, replica_groups=mesh['zl'=2,'y'=8,'co'=2,'zh'=4,'x'=4] {'zh','x'}, dimensions={0} | all-to-all | bytes 1769472 | tf_op jit(solution)/shard_map/all_to_all | solution.py:314
  88.6 0.7 shard_map.108.grad_ref.refs_2_
  89.3 0.3 copy-done.4
  89.6 0.9 shard_map.113
  90.5 14.9 %collective-permute-start.6 = (bf16[2560,128]{1,0:T(8,128)(2,1)S(1)}, bf16[2560,128]{1,0:T(8,128)(2,1)S(1)}, u32[]{:S(2)}, u32[]{:S(2)}) collective-permute-start(bf16[2560,128]{1,0:T(8,128)(2,1)S(1)} %shard_map.113), channel_id=1, source_target_pairs={{0,16},{16,0},{1,17},{17,1},{2,18},{18,2},{3,19},{19,3},{4,20},{20... | collective-permute-start | bytes 1966088 | tf_op jit(solution)/shard_map/ppermute | solution.py:260
  105.5 0.9 shard_map.112.kept_ref
  106.4 0.8 collective-permute-done.6.got_ref
  107.3 24.1 %all_to_all.21.slices_ref = bf16[16,160,128]{2,1,0:T(8,128)(2,1)S(1)} all-to-all(bf16[16,160,128]{2,1,0:T(8,128)(2,1)S(1)} %shard_map.114), channel_id=1, replica_groups=mesh['zl'=2,'y'=8,'co'=2,'zh'=4,'x'=4] {'zl','y'}, dimensions={0} | all-to-all | bytes 1310720 | tf_op jit(solution)/shard_map/all_to_all | solution.py:338
  131.5 22.9 %all_to_all.22 = bf16[16,160,128]{2,1,0:T(8,128)(2,1)S(1)} all-to-all(bf16[16,160,128]{2,1,0:T(8,128)(2,1)S(1)} %shard_map.115), channel_id=1, replica_groups=mesh['zl'=2,'y'=8,'co'=2,'zh'=4,'x'=4] {'zl','y'}, dimensions={0} | all-to-all | bytes 1310720 | tf_op jit(solution)/shard_map/all_to_all | solution.py:363
  154.4 5.4 %collective-permute-start.7 = (bf16[2560,128]{1,0:T(8,128)(2,1)S(1)}, bf16[2560,128]{1,0:T(8,128)(2,1)S(1)}, u32[]{:S(2)}, u32[]{:S(2)}) collective-permute-start(bf16[2560,128]{1,0:T(8,128)(2,1)S(1)} %bitcast.13), channel_id=1, source_target_pairs={{0,16},{16,0},{1,17},{17,1},{2,18},{18,2},{3,19},{19,3},{4,20},{20... | collective-permute-start | bytes 1966088 | tf_op jit(solution)/shard_map/ppermute | solution.py:260
  159.8 0.7 shard_map.109
  160.6 2.1 %collective-permute-start = (bf16[4,24,1152]{2,1,0:T(8,128)(2,1)S(1)}, bf16[4,24,1152]{2,1,0:T(8,128)(2,1)S(1)}, u32[]{:S(2)}, u32[]{:S(2)}) collective-permute-start(bf16[4,24,1152]{2,1,0:T(8,128)(2,1)S(1)} %get-tuple-element.31), channel_id=1, source_target_pairs={{0,1},{1,2},{2,3},{3,0},{4,5},{5,6},{6,7},{7,4},{8,9},{9,10},{10,1... | collective-permute-start | bytes 663560 | tf_op jit(solution)/shard_map/ppermute | solution.py:260
  162.6 3.8 %collective-permute-start.1 = (bf16[4,24,1152]{2,1,0:T(8,128)(2,1)S(1)}, bf16[4,24,1152]{2,1,0:T(8,128)(2,1)S(1)}, u32[]{:S(2)}, u32[]{:S(2)}) collective-permute-start(bf16[4,24,1152]{2,1,0:T(8,128)(2,1)S(1)} %get-tuple-element.32), channel_id=1, source_target_pairs={{0,2},{1,3},{2,0},{3,1},{4,6},{5,7},{6,4},{7,5},{8,10},{9,11},{10,... | collective-permute-start | bytes 663560 | tf_op jit(solution)/shard_map/ppermute | solution.py:260
  166.5 3.3 %collective-permute-start.2 = (bf16[4,24,1152]{2,1,0:T(8,128)(2,1)S(1)}, bf16[4,24,1152]{2,1,0:T(8,128)(2,1)S(1)}, u32[]{:S(2)}, u32[]{:S(2)}) collective-permute-start(bf16[4,24,1152]{2,1,0:T(8,128)(2,1)S(1)} %get-tuple-element.33), channel_id=1, source_target_pairs={{0,3},{1,0},{2,1},{3,2},{4,7},{5,4},{6,5},{7,6},{8,11},{9,8},{10,9... | collective-permute-start | bytes 663560 | tf_op jit(solution)/shard_map/ppermute | solution.py:260
  169.8 5.6 %collective-permute-done.k1 = bf16[4,24,1152]{2,1,0:T(8,128)(2,1)S(1)} collective-permute-done((bf16[4,24,1152]{2,1,0:T(8,128)(2,1)S(1)}, bf16[4,24,1152]{2,1,0:T(8,128)(2,1)S(1)}, u32[]{:S(2)}, u32[]{:S(2)}) %collective-permute-start) | collective-permute-done | bytes 221216 | tf_op jit(solution)/shard_map/ppermute | solution.py:260
  175.4 2.2 %collective-permute-done.2.k3 = bf16[4,24,1152]{2,1,0:T(8,128)(2,1)S(1)} collective-permute-done((bf16[4,24,1152]{2,1,0:T(8,128)(2,1)S(1)}, bf16[4,24,1152]{2,1,0:T(8,128)(2,1)S(1)}, u32[]{:S(2)}, u32[]{:S(2)}) %collective-permute-start.2) | collective-permute-done | bytes 221216 | tf_op jit(solution)/shard_map/ppermute | solution.py:260
  177.8 3.0 %collective-permute-start.3 = (bf16[24,1152]{1,0:T(8,128)(2,1)S(1)}, bf16[24,1152]{1,0:T(8,128)(2,1)S(1)}, u32[]{:S(2)}, u32[]{:S(2)}) collective-permute-start(bf16[24,1152]{1,0:T(8,128)(2,1)S(1)} %get-tuple-element.35), channel_id=1, source_target_pairs={{0,4},{4,8},{8,12},{12,0},{1,5},{5,9},{9,13},{13,1},{2,6},{6,10},{... | collective-permute-start | bytes 165896 | tf_op jit(solution)/shard_map/ppermute | solution.py:260
  180.8 4.5 %collective-permute-start.4 = (bf16[24,1152]{1,0:T(8,128)(2,1)S(1)}, bf16[24,1152]{1,0:T(8,128)(2,1)S(1)}, u32[]{:S(2)}, u32[]{:S(2)}) collective-permute-start(bf16[24,1152]{1,0:T(8,128)(2,1)S(1)} %get-tuple-element.36), channel_id=1, source_target_pairs={{0,8},{4,12},{8,0},{12,4},{1,9},{5,13},{9,1},{13,5},{2,10},{6,14},... | collective-permute-start | bytes 165896 | tf_op jit(solution)/shard_map/ppermute | solution.py:260
  185.4 3.4 %collective-permute-start.5 = (bf16[24,1152]{1,0:T(8,128)(2,1)S(1)}, bf16[24,1152]{1,0:T(8,128)(2,1)S(1)}, u32[]{:S(2)}, u32[]{:S(2)}) collective-permute-start(bf16[24,1152]{1,0:T(8,128)(2,1)S(1)} %get-tuple-element.37), channel_id=1, source_target_pairs={{0,12},{4,0},{8,4},{12,8},{1,13},{5,1},{9,5},{13,9},{2,14},{6,2},{... | collective-permute-start | bytes 165896 | tf_op jit(solution)/shard_map/ppermute | solution.py:260
  188.8 0.8 collective-permute-done.4.g2
  189.6 3.5 %collective-permute-done.5.g3 = bf16[24,1152]{1,0:T(8,128)(2,1)S(1)} collective-permute-done((bf16[24,1152]{1,0:T(8,128)(2,1)S(1)}, bf16[24,1152]{1,0:T(8,128)(2,1)S(1)}, u32[]{:S(2)}, u32[]{:S(2)}) %collective-permute-start.5) | collective-permute-done | bytes 55328 | tf_op jit(solution)/shard_map/ppermute | solution.py:260
  193.1 0.9 shard_map.111
  194.1 1.6 shard_map.116
  (32 shorter events, 0.7 us)
Async XLA Ops:
  0.6 33.8 %copy-start = (bf16[269,1152]{1,0:T(8,128)(2,1)S(1)}, bf16[269,1152]{1,0:T(8,128)(2,1)}, u32[]{:S(2)}) copy-start(bf16[269,1152]{1,0:T(8,128)(2,1)} %w_out_ref.3) | copy-start | bytes 1859332
  0.6 33.8 %copy-start.1 = (bf16[1152,269]{0,1:T(8,128)(2,1)S(1)}, bf16[1152,269]{0,1:T(8,128)(2,1)}, u32[]{:S(2)}) copy-start(bf16[1152,269]{0,1:T(8,128)(2,1)} %param.11) | copy-start | bytes 1859332
  22.7 11.8 %copy-start.8 = (bf16[4,24,1280]{2,1,0:T(8,128)(2,1)}, bf16[4,24,1280]{2,1,0:T(8,128)(2,1)S(1)}, u32[]{:S(2)}) copy-start(bf16[4,24,1280]{2,1,0:T(8,128)(2,1)S(1)} %get-tuple-element.27) | copy-start | bytes 737284
  36.9 0.7 copy-start.3
  37.6 0.8 copy-start.5
  38.4 23.4 %copy-start.10 = (bf16[1,384,24]{1,2,0:T(8,128)(2,1)S(1)}, bf16[1,384,24]{1,2,0:T(8,128)(2,1)}, u32[]{:S(2)}) copy-start(bf16[1,384,24]{1,2,0:T(8,128)(2,1)} %param.15) | copy-start | bytes 55300
  38.4 23.5 %copy-start.12 = (s32[24]{0:T(128)S(1)}, s32[24]{0:T(128)}, u32[]{:S(2)}) copy-start(s32[24]{0:T(128)} %param.14) | copy-start | bytes 292
  38.4 23.7 %all-to-all-start = ((bf16[16,24,1152]{2,1,0:T(8,128)(2,1)}), bf16[16,24,1152]{2,1,0:T(8,128)(2,1)S(1)}, u32[]{:S(2)}, u32[]{:S(2)}) async-start(bf16[16,24,1152]{2,1,0:T(8,128)(2,1)} %get-tuple-element.26), calls=%async_computation | async-start | bytes 1769472 | tf_op jit(solution)/shard_map/all_to_all | solution.py:310
  45.1 17.0 %copy-start.7 = (bf16[24,1152]{1,0:T(8,128)(2,1)S(1)}, bf16[24,1152]{1,0:T(8,128)(2,1)}, u32[]{:S(2)}) copy-start(bf16[24,1152]{1,0:T(8,128)(2,1)} %hidden_ref.3) | copy-start | bytes 165892
  45.1 17.0 %copy-start.11 = (f32[1152]{0:T(1024)S(1)}, f32[1152]{0:T(1024)}, u32[]{:S(2)}) copy-start(f32[1152]{0:T(1024)} %gain_ref.2) | copy-start | bytes 13828
  63.4 25.2 %copy-start.6 = (f32[384,269]{1,0:T(8,128)S(1)}, f32[384,269]{1,0:T(8,128)}, u32[]{:S(2)}) copy-start(f32[384,269]{1,0:T(8,128)} %copy-done.5) | copy-start | bytes 1239556
  88.6 1.0 copy-start.4
  90.5 16.6 %collective-permute-start.6 = (bf16[2560,128]{1,0:T(8,128)(2,1)S(1)}, bf16[2560,128]{1,0:T(8,128)(2,1)S(1)}, u32[]{:S(2)}, u32[]{:S(2)}) collective-permute-start(bf16[2560,128]{1,0:T(8,128)(2,1)S(1)} %shard_map.113), channel_id=1, source_target_pairs={{0,16},{16,0},{1,17},{17,1},{2,18},{18,2},{3,19},{19,3},{4,20},{20... | collective-permute-start | bytes 1966088 | tf_op jit(solution)/shard_map/ppermute | solution.py:260
  131.4 28.5 %copy-start.2 = (bf16[1152,269]{0,1:T(8,128)(2,1)S(1)}, bf16[1152,269]{0,1:T(8,128)(2,1)}, u32[]{:S(2)}) copy-start(bf16[1152,269]{0,1:T(8,128)(2,1)} %param.11) | copy-start | bytes 1859332
  131.5 61.7 %copy-start.9 = (f32[1152]{0:T(1024)S(1)}, f32[1152]{0:T(1024)}, u32[]{:S(2)}) copy-start(f32[1152]{0:T(1024)} %gain_ref.3) | copy-start | bytes 13828
  154.4 39.7 %collective-permute-start.7 = (bf16[2560,128]{1,0:T(8,128)(2,1)S(1)}, bf16[2560,128]{1,0:T(8,128)(2,1)S(1)}, u32[]{:S(2)}, u32[]{:S(2)}) collective-permute-start(bf16[2560,128]{1,0:T(8,128)(2,1)S(1)} %bitcast.13), channel_id=1, source_target_pairs={{0,16},{16,0},{1,17},{17,1},{2,18},{18,2},{3,19},{19,3},{4,20},{20... | collective-permute-start | bytes 1966088 | tf_op jit(solution)/shard_map/ppermute | solution.py:260
  160.6 14.8 %collective-permute-start = (bf16[4,24,1152]{2,1,0:T(8,128)(2,1)S(1)}, bf16[4,24,1152]{2,1,0:T(8,128)(2,1)S(1)}, u32[]{:S(2)}, u32[]{:S(2)}) collective-permute-start(bf16[4,24,1152]{2,1,0:T(8,128)(2,1)S(1)} %get-tuple-element.31), channel_id=1, source_target_pairs={{0,1},{1,2},{2,3},{3,0},{4,5},{5,6},{6,7},{7,4},{8,9},{9,10},{10,1... | collective-permute-start | bytes 663560 | tf_op jit(solution)/shard_map/ppermute | solution.py:260
  162.6 12.8 %collective-permute-start.1 = (bf16[4,24,1152]{2,1,0:T(8,128)(2,1)S(1)}, bf16[4,24,1152]{2,1,0:T(8,128)(2,1)S(1)}, u32[]{:S(2)}, u32[]{:S(2)}) collective-permute-start(bf16[4,24,1152]{2,1,0:T(8,128)(2,1)S(1)} %get-tuple-element.32), channel_id=1, source_target_pairs={{0,2},{1,3},{2,0},{3,1},{4,6},{5,7},{6,4},{7,5},{8,10},{9,11},{10,... | collective-permute-start | bytes 663560 | tf_op jit(solution)/shard_map/ppermute | solution.py:260
  166.5 11.1 %collective-permute-start.2 = (bf16[4,24,1152]{2,1,0:T(8,128)(2,1)S(1)}, bf16[4,24,1152]{2,1,0:T(8,128)(2,1)S(1)}, u32[]{:S(2)}, u32[]{:S(2)}) collective-permute-start(bf16[4,24,1152]{2,1,0:T(8,128)(2,1)S(1)} %get-tuple-element.33), channel_id=1, source_target_pairs={{0,3},{1,0},{2,1},{3,2},{4,7},{5,4},{6,5},{7,6},{8,11},{9,8},{10,9... | collective-permute-start | bytes 663560 | tf_op jit(solution)/shard_map/ppermute | solution.py:260
  177.8 11.0 %collective-permute-start.3 = (bf16[24,1152]{1,0:T(8,128)(2,1)S(1)}, bf16[24,1152]{1,0:T(8,128)(2,1)S(1)}, u32[]{:S(2)}, u32[]{:S(2)}) collective-permute-start(bf16[24,1152]{1,0:T(8,128)(2,1)S(1)} %get-tuple-element.35), channel_id=1, source_target_pairs={{0,4},{4,8},{8,12},{12,0},{1,5},{5,9},{9,13},{13,1},{2,6},{6,10},{... | collective-permute-start | bytes 165896 | tf_op jit(solution)/shard_map/ppermute | solution.py:260
  180.8 8.8 %collective-permute-start.4 = (bf16[24,1152]{1,0:T(8,128)(2,1)S(1)}, bf16[24,1152]{1,0:T(8,128)(2,1)S(1)}, u32[]{:S(2)}, u32[]{:S(2)}) collective-permute-start(bf16[24,1152]{1,0:T(8,128)(2,1)S(1)} %get-tuple-element.36), channel_id=1, source_target_pairs={{0,8},{4,12},{8,0},{12,4},{1,9},{5,13},{9,1},{13,5},{2,10},{6,14},... | collective-permute-start | bytes 165896 | tf_op jit(solution)/shard_map/ppermute | solution.py:260
  185.4 7.7 %collective-permute-start.5 = (bf16[24,1152]{1,0:T(8,128)(2,1)S(1)}, bf16[24,1152]{1,0:T(8,128)(2,1)S(1)}, u32[]{:S(2)}, u32[]{:S(2)}) collective-permute-start(bf16[24,1152]{1,0:T(8,128)(2,1)S(1)} %get-tuple-element.37), channel_id=1, source_target_pairs={{0,12},{4,0},{8,4},{12,8},{1,13},{5,1},{9,5},{13,9},{2,14},{6,2},{... | collective-permute-start | bytes 165896 | tf_op jit(solution)/shard_map/ppermute | solution.py:260

commit v5 on v4

--- a/solution.py
+++ b/solution.py
@@ -130,17 +130,15 @@
     target_ref[...] = same + 0.5 * jax.nn.sigmoid(teacher)
 
 
-def forward(all_ref, w_in_ref, w_out_ref, part_ref, act_ref, slope_ref, rows_ref):
+def forward(all_ref, w_in_ref, w_out_ref, part_ref):
     blocks, rows, width = part_ref.shape
+    pre_act = dot(all_ref[...].reshape(blocks * rows, width), w_in_ref[...], NT)
+    value, _ = gelu_both(pre_act)
+    part = dot(value.astype(BF16), w_out_ref[...], NN).astype(BF16)
+    part = part.reshape(blocks, rows, width)
     for x in range(4):
         for z in range(4):
-            rows_ref[z * 4 + x] = all_ref[x, z]
-    pre_act = dot(rows_ref[...].reshape(blocks * rows, width), w_in_ref[...], NT)
-    value, slope = gelu_both(pre_act)
-    act = value.astype(BF16)
-    act_ref[...] = act
-    slope_ref[...] = slope
-    part_ref[...] = dot(act, w_out_ref[...], NN).astype(BF16).reshape(blocks, rows, width)
+            part_ref[z * 4 + x] = part[x * 4 + z]
 
 
 def middle(part_ref, hidden_ref, gain_ref, image_ref, target_ref, out_ref, grad_ref):
@@ -162,15 +160,17 @@
     grad_final = (text_grad - unit * radial) / length
     grad = norm_backward(grad_final * gain, normed, inverse)
     grad_ref[...] = grad
-    sent = grad.astype(BF16)
-    for k in range(blocks):
-        out_ref[k] = sent
-
-
-def backward(rows_ref, w_out_ref, slope_ref, grad_ref):
-    blocks, rows, width = rows_ref.shape
-    grad_act = dot(rows_ref[...].reshape(blocks * rows, width), w_out_ref[...], NT)
-    grad_ref[...] = (grad_act * slope_ref[...]).astype(BF16)
+    out_ref[...] = grad.astype(BF16)
+
+
+def backward(all_ref, w_in_ref, rows_ref, w_out_ref, grad_ref, act_ref):
+    sides, _, rows, width = rows_ref.shape
+    group = sides * sides * rows
+    pre_act = dot(all_ref[...].reshape(group, width), w_in_ref[...], NT)
+    value, slope = gelu_both(pre_act)
+    act_ref[...] = value.astype(BF16)
+    grad_act = dot(rows_ref[...].reshape(group, width), w_out_ref[...], NT)
+    grad_ref[...] = (grad_act * slope).astype(BF16)
 
 
 def input_grad(grad_ref, w_in_ref, k0, k1, k2, k3, held):
@@ -179,23 +179,25 @@
     for k, out in enumerate((k0, k1, k2, k3)):
         x = lax.rem(at + k, 4)
         for z in range(4):
-            out[z] = held[z * 4 + x]
+            out[z] = held[x * 4 + z]
 
 
 def packed(a_ref, b_ref, out_ref, units, step, width):
     a = a_ref[...]
-    b = b_ref[...]
-    b = b.reshape(a.shape[0], width)
+    full = dot(a, b_ref[...].reshape(a.shape[0], width), TN).astype(out_ref.dtype)
     for c in range(width // LANES):
-        tile = dot(a, b[:, c * LANES : (c + 1) * LANES], TN)
-        out_ref[pl.ds(c * step, units), :] = tile.astype(out_ref.dtype)
+        out_ref[pl.ds(c * step, units), :] = full[:, c * LANES : (c + 1) * LANES]
 
 
 def weight_grad(first, step, act_ref, grads_ref, pre_ref, rows_ref, out_ref):
     units = act_ref.shape[1]
-    width = grads_ref.shape[2]
+    width = grads_ref.shape[-1]
     core = lax.axis_index("co")
-    out_ref[...] = jnp.zeros_like(out_ref)
+    blocks = width // LANES
+    for c in range(blocks):
+        start = c * step + units // 8 * 8
+        stop = (c + 1) * step if c + 1 < blocks else out_ref.shape[0]
+        out_ref[start:stop, :] = jnp.zeros((stop - start, LANES), out_ref.dtype)
 
     @pl.when(core == first)
     def _():
@@ -240,19 +242,30 @@
         spread(mine_ref, w_in_ref)
 
 
-def column_sum(k0, k1, k2, k3, keep_ref, s1, s2, s3, held):
-    at = lax.axis_index("zh")
+def column_sum(k0, k1, k2, k3, keep_ref, sent_ref, held):
+    half = lax.axis_index("zh") // 2
     total = k0[...].astype(F32) + k1[...].astype(F32)
     held[...] = total + k2[...].astype(F32) + k3[...].astype(F32)
-    keep_ref[...] = held[at]
-    for k, out in enumerate((s1, s2, s3)):
-        out[...] = held[lax.rem(at + k + 1, 4)].astype(BF16)
-
-
-def last(keep_ref, g1, g2, g3, hidden_ref, gain_ref, grad_ref, out_ref):
-    total = keep_ref[...] + g1[...].astype(F32) + g2[...].astype(F32) + g3[...].astype(F32)
+    for k in range(2):
+        keep_ref[k] = held[half * 2 + k]
+        sent_ref[k] = held[(1 - half) * 2 + k].astype(BF16)
+
+
+def pair_sum(kept_ref, got_ref, keep_ref, sent_ref):
+    side = lax.rem(lax.axis_index("zh"), 2)
+    keep_ref[...] = kept_ref[side] + got_ref[side].astype(F32)
+    sent_ref[...] = (kept_ref[1 - side] + got_ref[1 - side].astype(F32)).astype(BF16)
+
+
+def last(keep_ref, got_ref, hidden_ref, gain_ref, grad_ref, out_ref):
+    total = keep_ref[...] + got_ref[...].astype(F32)
     normed, inverse = norm_parts(hidden_ref[...].astype(F32))
     out_ref[...] = grad_ref[...] + norm_backward(total * gain_ref[...].reshape(1, -1), normed, inverse)
+
+
+def swap(value, axis, by):
+    length = lax.axis_size(axis)
+    return lax.ppermute(value, axis, [(i, i ^ by) for i in range(length)])
 
 
 def shift(value, axis, by):
@@ -295,25 +308,30 @@
     rows_column, column = call(
         split, [shape((4, rows, width), BF16), shape((4, rows, width + LANES), BF16)], both
     )
-    everything = lax.all_gather(rows_column, "x")
-    part, act, slope, group_input = call(
-        forward,
-        [spread, shape((group, units), BF16), shape((group, units), F32), spread],
-        everything,
-        w_in_rows,
-        w_out,
-        flops=2 * matmul,
-    )
+    group_input = lax.all_gather(rows_column, "x")
+    (part,) = call(forward, [spread], group_input, w_in_rows, w_out, flops=2 * matmul)
     part, column = lax.optimization_barrier((part, column))
     images = lax.all_gather(column, "x")
     (target,) = call(targets, [shape((rows, group), F32)], images, teacher, ids)
     parts = lax.all_to_all(part, BLK, 0, 0)
-    copies, grad_residual = call(
-        middle, [spread, shape((rows, width), F32)], parts, hidden_in, gain_final, images, target
-    )
-    group_grads = lax.all_to_all(copies, BLK, 0, 0)
-    (grad_pre,) = call(
-        backward, [shape((group, units), BF16)], group_grads, w_out, slope, flops=matmul
+    own_grads, grad_residual = call(
+        middle,
+        [shape((rows, width), BF16), shape((rows, width), F32)],
+        parts,
+        hidden_in,
+        gain_final,
+        images,
+        target,
+    )
+    group_grads = lax.all_gather(lax.all_gather(own_grads, "zh"), "x")
+    grad_pre, act = call(
+        backward,
+        [shape((group, units), BF16)] * 2,
+        group_input,
+        w_in_rows,
+        group_grads,
+        w_out,
+        flops=2 * matmul,
     )
 
     step = -(-units // 16) * 16
@@ -346,17 +364,21 @@
         flops=matmul,
         scratch=[pltpu.VMEM((blocks, rows, width), BF16)],
     )
-    arrived = [shift(s, "x", k + 1) for k, s in enumerate((s1, s2, s3))]
-    own, s1, s2, s3 = call(
+    arrived = []
+    for k, sent in ((1, s1), (2, s2), (3, s3)):
+        arrived.append(shift(sent, "x", k))
+    kept, sent = call(
         column_sum,
-        [shape((rows, width), F32)] + [shape((rows, width), BF16)] * 3,
+        [shape((2, rows, width), F32), shape((2, rows, width), BF16)],
         k0,
         *arrived,
         scratch=[pltpu.VMEM((4, rows, width), F32)],
     )
-    arrived = [shift(s, "zh", k + 1) for k, s in enumerate((s1, s2, s3))]
+    got = swap(sent, "zh", 2)
+    own, sent = call(pair_sum, [shape((rows, width), F32), shape((rows, width), BF16)], kept, got)
+    got = swap(sent, "zh", 1)
     (grad_hidden,) = call(
-        last, [shape((rows, width), F32)], own, *arrived, hidden_in, gain_mlp, grad_residual
+        last, [shape((rows, width), F32)], own, got, hidden_in, gain_mlp, grad_residual
     )
 
     (copies,) = call(ring_sum, [shape((ring, chunk, LANES), BF16)], slices)

time: 197 us -> 201 us (1.020); the launches traced: 196 us -> 198 us
  starting transfers between devices: 47.2 us -> 40.8 us
  blocking collectives: 121 us -> 126 us
  waiting for transfers between devices: 12.9 us -> 17.8 us
    all_gather x1 -> x3, blocking collectives: 11.8 us -> 38.1 us  [the longest x2 26.3 us: per_device(): group_grads = lax.all_gather(lax.all_gather(own_grads, 'zh'), 'x')]
    all_to_all x1 -> x0, blocking collectives: 25.2 us -> none  [per_device(): group_grads = lax.all_to_all(copies, BLK, 0, 0)]
    ppermute x8 -> x5, starting transfers between devices: 40.5 us -> 27.4 us  [shift(): lax.ppermute(value, axis, [(i, (i + by) % length) for i in range(length)])]
    ppermute x0 -> x2, waiting for transfers between devices: none -> 8.58 us  [swap(): return lax.ppermute(value, axis, [(i, i ^ by) for i in range(length)])]
    ppermute x0 -> x2, starting transfers between devices: none -> 6.7 us  [swap(): return lax.ppermute(value, axis, [(i, i ^ by) for i in range(length)])]
    all_to_all x1, blocking collectives: 24.1 us -> 28.1 us  [per_device(): slices = lax.all_to_all(mine, RING, 0, 0)]
    ppermute x8 -> x5, waiting for transfers between devices: 12.9 us -> 9.18 us  [shift(): lax.ppermute(value, axis, [(i, (i + by) % length) for i in range(length)])]
    pallas_call x14 -> x15, Pallas kernels: 11.9 us -> 11.6 us  [call(): pl.pallas_call(body, out_shape=tuple(outs), in_specs=[far if k in far_in...]
  transfers between devices with their start and end apart: 9 -> 8, of which waited for: 5 -> 6; matrix products, arithmetic and copies ran while one was open for 0% -> 0% of each run, Pallas kernels for 2% -> 1%
where the time goes in v5:
time: 201 us; the launch traced here: 198 us
  blocking collectives  126 us (63%)
  starting transfers between devices  40.8 us (20%)
  waiting for transfers between devices  17.8 us (9%)
  Pallas kernels  11.6 us (6%)
    all_to_all x1, blocking collectives, per_device(): slices = lax.all_to_all(mine, RING, 0, 0)  28.1 us
    ppermute x5, starting transfers between devices, shift(): lax.ppermute(value, axis, [(i, (i + by) % length) for i in range(length)])  27.4 us
    all_gather x2, blocking collectives, per_device(): group_grads = lax.all_gather(lax.all_gather(own_grads, 'zh'), 'x')  26.3 us
    all_to_all x1, blocking collectives, per_device(): whole = lax.all_to_all(copies, RING, 0, 0).reshape(tall, LANES)  22.8 us
    all_gather x1, blocking collectives, per_device(): both = lax.all_gather(own_rows, 'zh')  20.2 us
    all_gather x1, blocking collectives, per_device(): images = lax.all_gather(column, 'x')  16.7 us
    all_gather x1, blocking collectives, per_device(): group_input = lax.all_gather(rows_column, 'x')  11.7 us
    pallas_call x15, Pallas kernels, call(): pl.pallas_call(body, out_shape=tuple(outs), in_specs=[far if k in far_in...  11.6 us
  transfers between devices with their start and end apart: 8, of which 6 were waited for; matrix products, arithmetic and copies ran while one was open for 0% of the time, Pallas kernels for 1%

profile of v5, /device:TPU:1, one launch (start us, length us, event | category | flops | bytes accessed | tf_op | source)
XLA Modules:
  0.0 197.5 jit_solution(5624414386600631919)
XLA Ops:
  0.7 1.8 shard_map.103
  2.5 20.2 %all-gather = bf16[96,2432]{1,0:T(8,128)(2,1)S(1)} all-gather(bf16[24,2432]{1,0:T(8,128)(2,1)} %shard_map.103), channel_id=2, replica_groups=mesh['zl'=2,'y'=8,'co'=2,'zh'=4,'x'=4] {'zh'}, dimensions={0}, use_global_device_ids=true | all-gather | bytes 583680 | tf_op jit(solution)/shard_map/all_gather | solution.py:307
  22.7 0.7 copy-done.4
  23.4 11.7 %all-gather.1 = bf16[16,24,1152]{2,1,0:T(8,128)(2,1)S(1)} all-gather(bf16[4,24,1152]{2,1,0:T(8,128)(2,1)S(1)} %get-tuple-element.21), channel_id=3, replica_groups=mesh['zl'=2,'y'=8,'co'=2,'zh'=4,'x'=4] {'x'}, dimensions={0}, use_global_device_ids=true | all-gather | bytes 1105920 | tf_op jit(solution)/shard_map/all_gather | solution.py:311
  35.2 2.2 %shard_map.105 = bf16[16,24,1152]{2,1,0:T(8,128)(2,1)} custom-call(bf16[4,4,24,1152]{3,2,1,0:T(8,128)(2,1)S(1)} %bitcast.12, bf16[269,1152]{1,0:T(8,128)(2,1)S(1)} %bitcast.21, bf16[269,1152]{1,0:T(8,128)(2,1)S(1)} %copy-done.1), custom_call_target="tpu_custom_call" | custom-call | flops 475987968 | bytes 3009024 | tf_op jit(solution)/shard_map/pallas_call | solution.py:38
  37.4 6.6 %all-to-all-start = ((bf16[16,24,1152]{2,1,0:T(8,128)(2,1)}), bf16[16,24,1152]{2,1,0:T(8,128)(2,1)S(1)}, u32[]{:S(2)}, u32[]{:S(2)}) async-start(bf16[16,24,1152]{2,1,0:T(8,128)(2,1)} %shard_map.105), calls=%async_computation | async-start | bytes 1769472 | tf_op jit(solution)/shard_map/all_to_all | solution.py:316
  44.1 16.7 %all-gather.2 = bf16[16,24,1280]{2,1,0:T(8,128)(2,1)S(1)} all-gather(bf16[4,24,1280]{2,1,0:T(8,128)(2,1)} %copy-done.4), channel_id=4, replica_groups=mesh['zl'=2,'y'=8,'co'=2,'zh'=4,'x'=4] {'x'}, dimensions={0}, use_global_device_ids=true | all-gather | bytes 1228800 | tf_op jit(solution)/shard_map/all_gather | solution.py:314
  60.8 0.2 shard_map.106.target_ref
  61.1 1.2 shard_map.107
  62.3 15.1 %all-gather.3 = bf16[96,1152]{1,0:T(8,128)(2,1)S(1)} all-gather(bf16[24,1152]{1,0:T(8,128)(2,1)S(1)} %get-tuple-element.25), channel_id=5, replica_groups=mesh['zl'=2,'y'=8,'co'=2,'zh'=4,'x'=4] {'zh'}, dimensions={0}, use_global_device_ids=true | all-gather | bytes 276480 | tf_op jit(solution)/shard_map/all_gather | solution.py:326
  77.4 11.2 %all-gather.4 = bf16[16,24,1152]{2,1,0:T(8,128)(2,1)S(1)} all-gather(bf16[4,24,1152]{2,1,0:T(8,128)(2,1)S(1)} %bitcast.30), channel_id=6, replica_groups=mesh['zl'=2,'y'=8,'co'=2,'zh'=4,'x'=4] {'x'}, dimensions={0}, use_global_device_ids=true | all-gather | bytes 1105920 | tf_op jit(solution)/shard_map/all_gather | solution.py:326
  88.6 1.2 shard_map.108
  89.8 0.6 shard_map.114
  90.4 12.9 %collective-permute-start.5 = (bf16[2560,128]{1,0:T(8,128)(2,1)S(1)}, bf16[2560,128]{1,0:T(8,128)(2,1)S(1)}, u32[]{:S(2)}, u32[]{:S(2)}) collective-permute-start(bf16[2560,128]{1,0:T(8,128)(2,1)S(1)} %shard_map.114), channel_id=1, source_target_pairs={{0,16},{16,0},{1,17},{17,1},{2,18},{18,2},{3,19},{19,3},{4,20},{20... | collective-permute-start | bytes 1966088 | tf_op jit(solution)/shard_map/ppermute | solution.py:273
  103.3 0.6 shard_map.113.kept_ref
  103.9 1.1 collective-permute-done.5.got_ref
  105.1 28.1 %all_to_all.15.slices_ref = bf16[16,160,128]{2,1,0:T(8,128)(2,1)S(1)} all-to-all(bf16[16,160,128]{2,1,0:T(8,128)(2,1)S(1)} %shard_map.115), channel_id=1, replica_groups=mesh['zl'=2,'y'=8,'co'=2,'zh'=4,'x'=4] {'zl','y'}, dimensions={0} | all-to-all | bytes 1310720 | tf_op jit(solution)/shard_map/all_to_all | solution.py:356
  133.3 22.8 %all_to_all.16 = bf16[16,160,128]{2,1,0:T(8,128)(2,1)S(1)} all-to-all(bf16[16,160,128]{2,1,0:T(8,128)(2,1)S(1)} %shard_map.116), channel_id=1, replica_groups=mesh['zl'=2,'y'=8,'co'=2,'zh'=4,'x'=4] {'zl','y'}, dimensions={0} | all-to-all | bytes 1310720 | tf_op jit(solution)/shard_map/all_to_all | solution.py:385
  156.1 5.6 %collective-permute-start.6 = (bf16[2560,128]{1,0:T(8,128)(2,1)S(1)}, bf16[2560,128]{1,0:T(8,128)(2,1)S(1)}, u32[]{:S(2)}, u32[]{:S(2)}) collective-permute-start(bf16[2560,128]{1,0:T(8,128)(2,1)S(1)} %bitcast.24), channel_id=1, source_target_pairs={{0,16},{16,0},{1,17},{17,1},{2,18},{18,2},{3,19},{19,3},{4,20},{20... | collective-permute-start | bytes 1966088 | tf_op jit(solution)/shard_map/ppermute | solution.py:273
  161.7 0.7 shard_map.109
  162.4 1.9 collective-permute-start
  164.3 4.2 %collective-permute-start.1 = (bf16[4,24,1152]{2,1,0:T(8,128)(2,1)S(1)}, bf16[4,24,1152]{2,1,0:T(8,128)(2,1)S(1)}, u32[]{:S(2)}, u32[]{:S(2)}) collective-permute-start(bf16[4,24,1152]{2,1,0:T(8,128)(2,1)S(1)} %get-tuple-element.29), channel_id=1, source_target_pairs={{0,2},{1,3},{2,0},{3,1},{4,6},{5,7},{6,4},{7,5},{8,10},{9,11},{10,... | collective-permute-start | bytes 663560 | tf_op jit(solution)/shard_map/ppermute | solution.py:273
  168.6 2.8 %collective-permute-start.2 = (bf16[4,24,1152]{2,1,0:T(8,128)(2,1)S(1)}, bf16[4,24,1152]{2,1,0:T(8,128)(2,1)S(1)}, u32[]{:S(2)}, u32[]{:S(2)}) collective-permute-start(bf16[4,24,1152]{2,1,0:T(8,128)(2,1)S(1)} %get-tuple-element.30), channel_id=1, source_target_pairs={{0,3},{1,0},{2,1},{3,2},{4,7},{5,4},{6,5},{7,6},{8,11},{9,8},{10,9... | collective-permute-start | bytes 663560 | tf_op jit(solution)/shard_map/ppermute | solution.py:273
  171.4 1.4 collective-permute-done.k1
  172.8 4.1 %collective-permute-done.1.k2 = bf16[4,24,1152]{2,1,0:T(8,128)(2,1)S(1)} collective-permute-done((bf16[4,24,1152]{2,1,0:T(8,128)(2,1)S(1)}, bf16[4,24,1152]{2,1,0:T(8,128)(2,1)S(1)}, u32[]{:S(2)}, u32[]{:S(2)}) %collective-permute-start.1) | collective-permute-done | bytes 221216 | tf_op jit(solution)/shard_map/ppermute | solution.py:273
  176.9 2.5 %collective-permute-done.2.k3 = bf16[4,24,1152]{2,1,0:T(8,128)(2,1)S(1)} collective-permute-done((bf16[4,24,1152]{2,1,0:T(8,128)(2,1)S(1)}, bf16[4,24,1152]{2,1,0:T(8,128)(2,1)S(1)}, u32[]{:S(2)}, u32[]{:S(2)}) %collective-permute-start.2) | collective-permute-done | bytes 221216 | tf_op jit(solution)/shard_map/ppermute | solution.py:273
  179.7 4.3 %collective-permute-start.3 = (bf16[2,24,1152]{2,1,0:T(8,128)(2,1)S(1)}, bf16[2,24,1152]{2,1,0:T(8,128)(2,1)S(1)}, u32[]{:S(2)}, u32[]{:S(2)}) collective-permute-start(bf16[2,24,1152]{2,1,0:T(8,128)(2,1)S(1)} %get-tuple-element.32), channel_id=1, source_target_pairs={{0,8},{4,12},{8,0},{12,4},{1,9},{5,13},{9,1},{13,5},{2,10},{6,14},... | collective-permute-start | bytes 331784 | tf_op jit(solution)/shard_map/ppermute | solution.py:268
  183.9 5.2 %collective-permute-done.3.got_ref = bf16[2,24,1152]{2,1,0:T(8,128)(2,1)S(1)} collective-permute-done((bf16[2,24,1152]{2,1,0:T(8,128)(2,1)S(1)}, bf16[2,24,1152]{2,1,0:T(8,128)(2,1)S(1)}, u32[]{:S(2)}, u32[]{:S(2)}) %collective-permute-start.3) | collective-permute-done | bytes 110624 | tf_op jit(solution)/shard_map/ppermute | solution.py:268
  189.2 2.4 %collective-permute-start.4 = (bf16[24,1152]{1,0:T(8,128)(2,1)S(1)}, bf16[24,1152]{1,0:T(8,128)(2,1)S(1)}, u32[]{:S(2)}, u32[]{:S(2)}) collective-permute-start(bf16[24,1152]{1,0:T(8,128)(2,1)S(1)} %get-tuple-element.34), channel_id=1, source_target_pairs={{0,4},{4,0},{8,12},{12,8},{1,5},{5,1},{9,13},{13,9},{2,6},{6,2},{1... | collective-permute-start | bytes 165896 | tf_op jit(solution)/shard_map/ppermute | solution.py:268
  191.6 3.3 %collective-permute-done.4.got_ref = bf16[24,1152]{1,0:T(8,128)(2,1)S(1)} collective-permute-done((bf16[24,1152]{1,0:T(8,128)(2,1)S(1)}, bf16[24,1152]{1,0:T(8,128)(2,1)S(1)}, u32[]{:S(2)}, u32[]{:S(2)}) %collective-permute-start.4) | collective-permute-done | bytes 55328 | tf_op jit(solution)/shard_map/ppermute | solution.py:268
  195.0 0.9 shard_map.112
  195.9 1.6 shard_map.117
  (24 shorter events, 0.5 us)
Async XLA Ops:
  0.6 34.5 %copy-start.1 = (bf16[269,1152]{1,0:T(8,128)(2,1)S(1)}, bf16[269,1152]{1,0:T(8,128)(2,1)}, u32[]{:S(2)}) copy-start(bf16[269,1152]{1,0:T(8,128)(2,1)} %w_out_ref.3) | copy-start | bytes 1859332
  0.6 34.5 %copy-start = (bf16[1152,269]{0,1:T(8,128)(2,1)S(1)}, bf16[1152,269]{0,1:T(8,128)(2,1)}, u32[]{:S(2)}) copy-start(bf16[1152,269]{0,1:T(8,128)(2,1)} %param.11) | copy-start | bytes 1859332
  22.7 0.7 copy-start.4
  37.4 23.4 %copy-start.6 = (bf16[1,384,24]{1,2,0:T(8,128)(2,1)S(1)}, bf16[1,384,24]{1,2,0:T(8,128)(2,1)}, u32[]{:S(2)}) copy-start(bf16[1,384,24]{1,2,0:T(8,128)(2,1)} %param.15) | copy-start | bytes 55300
  37.4 23.4 %copy-start.8 = (s32[24]{0:T(128)S(1)}, s32[24]{0:T(128)}, u32[]{:S(2)}) copy-start(s32[24]{0:T(128)} %param.14) | copy-start | bytes 292
  37.4 23.7 %all-to-all-start = ((bf16[16,24,1152]{2,1,0:T(8,128)(2,1)}), bf16[16,24,1152]{2,1,0:T(8,128)(2,1)S(1)}, u32[]{:S(2)}, u32[]{:S(2)}) async-start(bf16[16,24,1152]{2,1,0:T(8,128)(2,1)} %shard_map.105), calls=%async_computation | async-start | bytes 1769472 | tf_op jit(solution)/shard_map/all_to_all | solution.py:316
  44.1 17.0 %copy-start.3 = (bf16[24,1152]{1,0:T(8,128)(2,1)S(1)}, bf16[24,1152]{1,0:T(8,128)(2,1)}, u32[]{:S(2)}) copy-start(bf16[24,1152]{1,0:T(8,128)(2,1)} %hidden_ref.3) | copy-start | bytes 165892
  44.1 17.0 %copy-start.7 = (f32[1152]{0:T(1024)S(1)}, f32[1152]{0:T(1024)}, u32[]{:S(2)}) copy-start(f32[1152]{0:T(1024)} %gain_ref.2) | copy-start | bytes 13828
  61.1 27.6 %copy-start.2 = (bf16[269,1152]{1,0:T(8,128)(2,1)S(1)}, bf16[269,1152]{1,0:T(8,128)(2,1)}, u32[]{:S(2)}) copy-start(bf16[269,1152]{1,0:T(8,128)(2,1)} %w_out_ref.3) | copy-start | bytes 1859332
  90.4 14.6 %collective-permute-start.5 = (bf16[2560,128]{1,0:T(8,128)(2,1)S(1)}, bf16[2560,128]{1,0:T(8,128)(2,1)S(1)}, u32[]{:S(2)}, u32[]{:S(2)}) collective-permute-start(bf16[2560,128]{1,0:T(8,128)(2,1)S(1)} %shard_map.114), channel_id=1, source_target_pairs={{0,16},{16,0},{1,17},{17,1},{2,18},{18,2},{3,19},{19,3},{4,20},{20... | collective-permute-start | bytes 1966088 | tf_op jit(solution)/shard_map/ppermute | solution.py:273
  156.1 38.9 %copy-start.5 = (f32[1152]{0:T(1024)S(1)}, f32[1152]{0:T(1024)}, u32[]{:S(2)}) copy-start(f32[1152]{0:T(1024)} %gain_ref.3) | copy-start | bytes 13828
  156.1 39.8 %collective-permute-start.6 = (bf16[2560,128]{1,0:T(8,128)(2,1)S(1)}, bf16[2560,128]{1,0:T(8,128)(2,1)S(1)}, u32[]{:S(2)}, u32[]{:S(2)}) collective-permute-start(bf16[2560,128]{1,0:T(8,128)(2,1)S(1)} %bitcast.24), channel_id=1, source_target_pairs={{0,16},{16,0},{1,17},{17,1},{2,18},{18,2},{3,19},{19,3},{4,20},{20... | collective-permute-start | bytes 1966088 | tf_op jit(solution)/shard_map/ppermute | solution.py:273
  162.4 10.4 %collective-permute-start = (bf16[4,24,1152]{2,1,0:T(8,128)(2,1)S(1)}, bf16[4,24,1152]{2,1,0:T(8,128)(2,1)S(1)}, u32[]{:S(2)}, u32[]{:S(2)}) collective-permute-start(bf16[4,24,1152]{2,1,0:T(8,128)(2,1)S(1)} %get-tuple-element.28), channel_id=1, source_target_pairs={{0,1},{1,2},{2,3},{3,0},{4,5},{5,6},{6,7},{7,4},{8,9},{9,10},{10,1... | collective-permute-start | bytes 663560 | tf_op jit(solution)/shard_map/ppermute | solution.py:273
  164.3 12.6 %collective-permute-start.1 = (bf16[4,24,1152]{2,1,0:T(8,128)(2,1)S(1)}, bf16[4,24,1152]{2,1,0:T(8,128)(2,1)S(1)}, u32[]{:S(2)}, u32[]{:S(2)}) collective-permute-start(bf16[4,24,1152]{2,1,0:T(8,128)(2,1)S(1)} %get-tuple-element.29), channel_id=1, source_target_pairs={{0,2},{1,3},{2,0},{3,1},{4,6},{5,7},{6,4},{7,5},{8,10},{9,11},{10,... | collective-permute-start | bytes 663560 | tf_op jit(solution)/shard_map/ppermute | solution.py:273
  168.6 10.9 %collective-permute-start.2 = (bf16[4,24,1152]{2,1,0:T(8,128)(2,1)S(1)}, bf16[4,24,1152]{2,1,0:T(8,128)(2,1)S(1)}, u32[]{:S(2)}, u32[]{:S(2)}) collective-permute-start(bf16[4,24,1152]{2,1,0:T(8,128)(2,1)S(1)} %get-tuple-element.30), channel_id=1, source_target_pairs={{0,3},{1,0},{2,1},{3,2},{4,7},{5,4},{6,5},{7,6},{8,11},{9,8},{10,9... | collective-permute-start | bytes 663560 | tf_op jit(solution)/shard_map/ppermute | solution.py:273
  179.7 9.5 %collective-permute-start.3 = (bf16[2,24,1152]{2,1,0:T(8,128)(2,1)S(1)}, bf16[2,24,1152]{2,1,0:T(8,128)(2,1)S(1)}, u32[]{:S(2)}, u32[]{:S(2)}) collective-permute-start(bf16[2,24,1152]{2,1,0:T(8,128)(2,1)S(1)} %get-tuple-element.32), channel_id=1, source_target_pairs={{0,8},{4,12},{8,0},{12,4},{1,9},{5,13},{9,1},{13,5},{2,10},{6,14},... | collective-permute-start | bytes 331784 | tf_op jit(solution)/shard_map/ppermute | solution.py:268
  189.2 5.8 %collective-permute-start.4 = (bf16[24,1152]{1,0:T(8,128)(2,1)S(1)}, bf16[24,1152]{1,0:T(8,128)(2,1)S(1)}, u32[]{:S(2)}, u32[]{:S(2)}) collective-permute-start(bf16[24,1152]{1,0:T(8,128)(2,1)S(1)} %get-tuple-element.34), channel_id=1, source_target_pairs={{0,4},{4,0},{8,12},{12,8},{1,5},{5,1},{9,13},{13,9},{2,6},{6,2},{1... | collective-permute-start | bytes 165896 | tf_op jit(solution)/shard_map/ppermute | solution.py:268
